TPU v7x, 32 devices: a whole 2x2x4 slice. The times are simulated.
32 devices in a mesh: section: 2 (over core), dp: 16 (over z, y, x).
Axes of the slice: x: 2, y: 2, z: 4, core: 2. Of those that a mesh axis runs over, the one named last changes fastest.
Arguments:
- tokens: bfloat16 [128, 256, 512], P('dp'), may hold values from -6 to 6
- out_cotangent: bfloat16 [128, 256, 512], P('dp'), may hold values from -8 to 8
- speaker: int32 [128], P('dp'), may hold values from 0 to 2559
- valid: int32 [128], P('dp'), may hold values 0 or 1
- conv_weight: float32 [2, 7, 512], P('section'), may hold values from -2 to 2
- conv_bias: float32 [2, 512], P('section'), may hold values from -3 to 3
- scale_table: float32 [2, 2560, 512], P('section'), may hold values from 0.1 to 1.9
- shift_table: float32 [2, 2560, 512], P('section'), may hold values from -3 to 3
- up_weight: bfloat16 [2, 512, 1536], P('section'), may hold values from -0.25 to 0.25
- up_bias: float32 [2, 1536], P('section'), may hold values from -3 to 3
- down_weight: bfloat16 [2, 1536, 512], P('section'), may hold values from -0.15625 to 0.15625
- down_bias: float32 [2, 512], P('section'), may hold values from -3 to 3
- layer_scale: float32 [2, 512], P('section'), may hold values from 0.5 to 1.5
Outputs:
- block_outputs: bfloat16 [2, 128, 256, 512], P('section', 'dp')
- input_grads: bfloat16 [2, 128, 256, 512], P('section', 'dp')
- grad_conv_weight: float32 [2, 7, 512], P('section', None, 'dp')
- grad_conv_bias: float32 [2, 512], P('section', 'dp')
- grad_scale_table: float32 [2, 2560, 512], P('section', 'dp')
- grad_shift_table: float32 [2, 2560, 512], P('section', 'dp')
- grad_up_weight: float32 [2, 512, 1536], P('section', 'dp')
- grad_up_bias: float32 [2, 1536], P('section', 'dp')
- grad_down_weight: float32 [2, 1536, 512], P('section', 'dp')
- grad_down_bias: float32 [2, 512], P('section', 'dp')
- grad_layer_scale: float32 [2, 512], P('section', 'dp')
All inputs are finite; a program needn't handle non-finite values. No bound on the sum of `valid` on one device may be relied on, other than what follows from the above.
Results may differ from a plain program's by a relative error of at most 0.0074.
Values may be sent and summed in bfloat16 or wider, within the bound.
No kernel may reach another device: no remote copies, remote signals or barrier semaphores. Data moves between devices by JAX's collectives and lax.ppermute only.
A program may use at most 192 MiB of HBM per device.

v0:
```python
import functools

import jax
import jax.numpy as jnp
from jax import lax
from jax.experimental import pallas as pl
from jax.experimental.pallas import tpu as pltpu
from jax.sharding import PartitionSpec as P


F32 = jnp.float32
BF16 = jnp.bfloat16
PAIR = ("section", "dp")
TILE = 512
ALL_VMEM = 67043328
HALF_ROOT = 0.7071067811865476
DENSITY = 0.3989422804014327
BLOCKS = 16
ORDERS = ((0, 1, 2, 3), (2, 0, 1, 3))
ANY = pl.BlockSpec(memory_space=pl.ANY)
HBM = pl.BlockSpec(memory_space=pltpu.HBM)
VMEM = pl.BlockSpec(memory_space=pltpu.VMEM)
SMEM = pl.BlockSpec(memory_space=pltpu.SMEM)

TAPS, CONV, UPB, DOWNB, GAIN, SCALE, SHIFT, SMALL = 0, 7, 8, 11, 12, 16, 20, 24


def position(block, order):
    place = 0
    for bit in order:
        place = 2 * place + ((block >> bit) & 1)
    return place


def dot(a, b, dims):
    return lax.dot_general(a, b, (dims, ((), ())), preferred_element_type=F32)


NN = ((1,), (0,))
NT = ((1,), (1,))
TN = ((0,), (0,))


OFFSETS = (-3, -2, -1, 1, 2, 3)


def set_shifts(shifts):
    frames = shifts.shape[1]
    row = lax.broadcasted_iota(jnp.int32, (frames, frames), 0)
    col = lax.broadcasted_iota(jnp.int32, (frames, frames), 1)
    for n, offset in enumerate(OFFSETS):
        shifts[n * frames : (n + 1) * frames] = jnp.where(col == row + offset, 1.0, 0.0).astype(BF16)


def shifted(shifts, x, offset):
    frames = x.shape[0]
    n = OFFSETS.index(offset)
    return dot(shifts[n * frames : (n + 1) * frames], x, NN)


def wide(x, width):
    return jnp.concatenate([x] * (width // 128), axis=1)


def rowsum(x):
    return jnp.sum(x, axis=0, keepdims=True)


def normalize(x, small, clip, shifts):
    conv = small[CONV : CONV + 1] + x.astype(F32) * small[3:4]
    for offset in OFFSETS:
        conv = conv + shifted(shifts, x, offset) * small[offset + 3 : offset + 4]
    centred = conv - jnp.mean(conv, axis=-1, keepdims=True)
    inv = lax.rsqrt(jnp.mean(centred * centred, axis=-1, keepdims=True) + 1e-06)
    normed = centred * inv
    scale = small[pl.ds(SCALE + clip, 1)]
    shift = small[pl.ds(SHIFT + clip, 1)]
    adapted = (normed * scale + shift).astype(BF16)
    return adapted, normed.astype(BF16), jnp.broadcast_to(inv, (x.shape[0], 128))


def prep_body(sec, speaker, taps, conv, upb, downb, gain, scale_hbm, shift_hbm, own, other, sems):
    width = own.shape[1]
    half = SMALL - SHIFT
    copies = []
    for side, out in enumerate((own, other)):
        first = (sec[0] if side == 0 else 1 - sec[0]) * half
        for clip in range(half):
            row = speaker[first + clip]
            for kind, table in enumerate((scale_hbm, shift_hbm)):
                copies.append(
                    pltpu.make_async_copy(
                        table.at[0, pl.ds(row, 1)],
                        out.at[pl.ds((SCALE, SHIFT)[kind] + clip, 1)],
                        sems.at[side, kind, clip],
                    )
                )
    for copy in copies:
        copy.start()
    for out in (own, other):
        for k in range(7):
            out[TAPS + k : TAPS + k + 1] = taps[k]
        out[CONV : CONV + 1] = conv[...]
        for k in range(DOWNB - UPB):
            out[UPB + k : UPB + k + 1] = upb[:, k * width : (k + 1) * width]
        out[DOWNB : DOWNB + 1] = downb[...]
        out[GAIN : GAIN + 1] = gain[...]
        out[GAIN + 1 : SCALE] = jnp.zeros((SCALE - GAIN - 1, width), F32)
    for copy in copies:
        copy.wait()


def forward_tiles(adapted, up, down, small, act, slope, acc):
    steps = [(j, r) for j in range(3) for r in range(acc.shape[0] // 256)]

    def hidden(j, r):
        part = dot(adapted[r * 256 : (r + 1) * 256], up[:, j * TILE : (j + 1) * TILE], NN)
        return part + small[UPB + j : UPB + j + 1]

    ahead = hidden(*steps[0])
    for n, (j, r) in enumerate(steps):
        rows = slice(r * 256, (r + 1) * 256)
        pre = ahead
        if n + 1 < len(steps):
            ahead = hidden(*steps[n + 1])
        phi = 0.5 * lax.erf(pre * HALF_ROOT) + 0.5
        low = (pre * phi).astype(BF16)
        act[j, rows] = low
        slope[j, rows] = (phi + pre * (DENSITY * jnp.exp(-0.5 * pre * pre))).astype(BF16)
        part = dot(low, down[j * TILE : (j + 1) * TILE], NN)
        acc[rows] = part if j == 0 else acc[rows] + part


def activation_tile(j, gb, down, slope, sums):
    total = jnp.zeros((1, TILE), F32)
    for r in range(gb.shape[0] // 256):
        rows = slice(r * 256, (r + 1) * 256)
        gact = dot(gb[rows], down[j * TILE : (j + 1) * TILE], NT)
        gpre = (gact * slope[j, rows].astype(F32)).astype(BF16)
        slope[j, rows] = gpre
        total = total + rowsum(gpre.astype(F32))
    sums[UPB + j : UPB + j + 1] = total


def down_pieces(j, order):
    share = 3 * TILE // BLOCKS
    at, pieces = j * TILE, []
    while at < (j + 1) * TILE:
        stop = min((at // share + 1) * share, (j + 1) * TILE)
        pieces.append((position(at // share, order), at % share, stop - at, at - j * TILE))
        at = stop
    return pieces


def up_tile(j, order, adapted, gpre, upd):
    gup = dot(adapted[...], gpre, TN).astype(BF16)
    share = TILE // BLOCKS
    for i in range(BLOCKS):
        upd[position(i, order), j * share : (j + 1) * share] = gup[i * share : (i + 1) * share]


def down_tile(j, order, gb, act, dnd):
    gdn = dot(act, gb[...], TN).astype(BF16)
    for block, first, rows, at in down_pieces(j, order):
        dnd[block, first : first + rows] = gdn[at : at + rows]


def norm_backward(gad, normed, inv, small, clip, grad_out, v, shifts):
    n = normed.astype(F32)
    width = n.shape[1]
    scale = small[pl.ds(SCALE + clip, 1)]
    g_shift = rowsum(gad)
    g_scale = rowsum(gad * n)
    gn = gad * scale
    m1 = jnp.mean(gn, axis=-1, keepdims=True)
    m2 = jnp.mean(gn * n, axis=-1, keepdims=True)
    gc = (gn - m1 - n * m2) * wide(inv, width)
    low = gc.astype(BF16)
    total = grad_out + gc * small[3:4]
    v = v.astype(F32)
    g_taps = []
    for k in range(7):
        if k == 3:
            g_taps.append(rowsum(gc * v))
            continue
        moved = shifted(shifts, low, 3 - k)
        total = total + moved * small[k : k + 1]
        g_taps.append(rowsum(moved * v))
    return total.astype(BF16), jnp.concatenate(g_taps + [rowsum(gc)], axis=0), g_scale, g_shift


def place_weights(sec, block, up_own, up_got, down_own, down_got, up, down, sems, start):
    def go(up_from, down_from):
        for source, target, sem in ((up_from, up, sems.at[0]), (down_from, down, sems.at[1])):
            copy = pltpu.make_async_copy(source, target, sem)
            copy.start() if start else copy.wait()

    if not start:
        go(up_own, down_own)
        return

    @pl.when(sec[0] == block)
    def _():
        go(up_own, down_own)

    @pl.when(sec[0] != block)
    def _():
        go(up_got, down_got)


def leaving(block, place):
    return 1 - ((place[0] >> ORDERS[block][0]) & 1)


def route_block(block, layer, sec, place, sums, kept, passed, stays, sems, start):
    half = BLOCKS // 2
    goes = leaving(block, place)

    def go(*targets):
        for side, (target, first) in enumerate(zip(targets, (goes, 1 - goes))):
            part = sums.at[pl.ds(first * half, half)]
            copy = pltpu.make_async_copy(part, target, sems.at[layer, side])
            copy.start() if start else copy.wait()

    if not start:
        go(passed, stays)
        return

    @pl.when(sec[0] == block)
    def _():
        go(kept.at[pl.ds(goes * half, half)], kept.at[pl.ds((1 - goes) * half, half)])

    @pl.when(sec[0] != block)
    def _():
        go(passed, stays)


def route(sec, upd, dnd, keep, send, sems, start):
    def go(kept, sent):
        for source, target, sem in ((kept, keep, sems.at[0]), (sent, send, sems.at[1])):
            copy = pltpu.make_async_copy(source, target, sem)
            copy.start() if start else copy.wait()

    if not start:
        go(upd, dnd)
        return

    @pl.when(sec[0] == 0)
    def _():
        go(upd, dnd)

    @pl.when(sec[0] != 0)
    def _():
        go(dnd, upd)


def main_body(
    sec, place, valid, own_small, got_small, tokens, cot, up_own, up_got, down_own, down_got,
    sums0, sums1, gin1, normed_hbm, inv_hbm, out_own, out_send, gpre_hbm, up_keep, down_keep,
    up_pass, down_pass, up_stay, down_stay, small0_out,
    up0, down0, up1, down1, act0, slope0, act1, slope1, acc, adapted0, normed, inv, adapted1, branch0,
    gb, v, grad, out0, out1, small0, small1, shifts, upd, dnd, upd0, dnd0, sems, pieces, parts,
):
    clips = acc.shape[0] // 256
    mine = pl.ds(sec[0] * clips, clips)
    loads = (
        pltpu.make_async_copy(tokens.at[mine], v, sems.at[6, 0]),
        pltpu.make_async_copy(cot.at[mine], grad, sems.at[6, 1]),
    )
    loads[0].start()
    weights = (up_own, up_got, down_own, down_got)
    place_weights(sec, 0, *weights, up0, down0, sems.at[0], True)
    place_weights(sec, 1, *weights, up1, down1, sems.at[1], True)
    loads[1].start()
    first = sec[0] == 0
    small0[...] = pick(first, own_small[...], got_small[...])
    small1[...] = pick(first, got_small[...], own_small[...])
    small0_out[...] = small0[...]
    sums0[...] = jnp.zeros_like(sums0)
    sums1[...] = jnp.zeros_like(sums1)
    set_shifts(shifts)
    loads[0].wait()

    def begin(r):
        rows = pl.ds(pl.multiple_of(r * 256, 256), 256)
        adapted0[rows], normed[rows], inv[rows] = normalize(v[r], small0, r, shifts)

    pl.loop(0, clips, unroll=True)(begin)
    saves = [
        pltpu.make_async_copy(source, target, sems.at[7 + n // 2, n % 2])
        for n, (source, target) in enumerate(
            ((normed, normed_hbm), (inv, inv_hbm))
        )
    ]
    for copy in saves:
        copy.start()
    place_weights(sec, 0, *weights, up0, down0, sems.at[0], False)
    forward_tiles(adapted0, up0, down0, small0, act0, slope0, acc)
    for copy in saves:
        copy.wait()

    def between(r):
        rows = pl.ds(pl.multiple_of(r * 256, 256), 256)
        branch = acc[rows] + small0[DOWNB : DOWNB + 1]
        branch0[rows] = branch
        result = (v[r].astype(F32) + small0[GAIN : GAIN + 1] * branch).astype(BF16)
        out0[r] = result
        adapted1[rows], normed[rows], inv[rows] = normalize(result, small1, r, shifts)

    pl.loop(0, clips, unroll=True)(between)
    place_weights(sec, 1, *weights, up1, down1, sems.at[1], False)
    forward_tiles(adapted1, up1, down1, small1, act1, slope1, acc)
    loads[1].wait()

    def top(r):
        rows = pl.ds(pl.multiple_of(r * 256, 256), 256)
        branch = acc[rows] + small1[DOWNB : DOWNB + 1]
        gain = small1[GAIN : GAIN + 1]
        out1[r] = (out0[r].astype(F32) + gain * branch).astype(BF16)
        above = grad[r].astype(F32) * valid[sec[0] * clips + r].astype(F32)
        low = (above * gain).astype(BF16)
        gb[rows] = low
        sums1[GAIN : GAIN + 1] += rowsum(above * branch)
        sums1[DOWNB : DOWNB + 1] += rowsum(low.astype(F32))

    pl.loop(0, clips)(top)
    half_own = out_own.at[mine]
    route(sec, out0, out1, half_own, out_send, sems.at[4], True)
    for j in range(3):
        activation_tile(j, gb, down1, slope1, sums1)
        for r in range(clips):
            rows = slice(r * 256, (r + 1) * 256)
            part = dot(slope1[j, rows], up1[:, j * TILE : (j + 1) * TILE], NT)
            acc[rows] = part if j == 0 else acc[rows] + part
        up_tile(j, ORDERS[1], adapted1, slope1[j], upd)
        down_tile(j, ORDERS[1], gb, act1[j], dnd)
    ends = ((up_keep, up_pass, up_stay), (down_keep, down_pass, down_stay))
    for n, source in enumerate((upd, dnd)):
        route_block(1, n, sec, place, source, *ends[n], parts.at[1], True)

    def move(r):
        return pltpu.make_async_copy(grad.at[r], gin1.at[r], pieces.at[r])

    def under(r):
        rows = pl.ds(pl.multiple_of(r * 256, 256), 256)
        above = grad[r].astype(F32) * valid[sec[0] * clips + r].astype(F32)
        gin, smalls, g_scale, g_shift = norm_backward(
            acc[rows], normed[rows], inv[rows], small1, r, above, out0[r], shifts
        )
        grad[r] = gin
        sums1[TAPS : TAPS + 8] += smalls
        sums1[pl.ds(SCALE + r, 1)] = g_scale
        sums1[pl.ds(SHIFT + r, 1)] = g_shift
        grad0 = gin.astype(F32)
        low = (grad0 * small0[GAIN : GAIN + 1]).astype(BF16)
        gb[rows] = low
        move(r).start()
        sums0[GAIN : GAIN + 1] += rowsum(grad0 * branch0[rows])
        sums0[DOWNB : DOWNB + 1] += rowsum(low.astype(F32))

    pl.loop(0, clips, unroll=True)(under)
    tiles = []
    for j in range(3):
        activation_tile(j, gb, down0, slope0, sums0)
        tiles.append(pltpu.make_async_copy(slope0.at[j], gpre_hbm.at[j], sems.at[5 + j // 2 * 3, j % 2]))
        tiles[-1].start()
        up_tile(j, ORDERS[0], adapted0, slope0[j], upd0)
    route_block(0, 0, sec, place, upd0, *ends[0], parts.at[0], True)
    for j in range(3):
        down_tile(j, ORDERS[0], gb, act0[j], dnd0)
    route_block(0, 1, sec, place, dnd0, *ends[1], parts.at[0], True)
    route(sec, out0, out1, half_own, out_send, sems.at[4], False)
    for n, source in enumerate((upd, dnd)):
        route_block(1, n, sec, place, source, *ends[n], parts.at[1], False)
    for copy in tiles + [move(r) for r in range(clips)]:
        copy.wait()
    for n, source in enumerate((upd0, dnd0)):
        route_block(0, n, sec, place, source, *ends[n], parts.at[0], False)


def last_body(
    sec, gpre, up_own, up_got, normed, inv, small, grad_out, tokens, sums0, sums1, gin, away, own, send,
    up, shifts, sums, sem,
):
    clip = pl.program_id(0)

    @pl.when(clip == 0)
    def _():
        sums[...] = sums0[...]

        @pl.when(sec[0] == 0)
        def _():
            pltpu.make_async_copy(up_own, up, sem).start()

        @pl.when(sec[0] != 0)
        def _():
            pltpu.make_async_copy(up_got, up, sem).start()

        set_shifts(shifts)
        pltpu.make_async_copy(up_own, up, sem).wait()

    gad = dot(gpre[0], up[:, :TILE], NT)
    for j in range(1, 3):
        gad = gad + dot(gpre[j], up[:, j * TILE : (j + 1) * TILE], NT)
    above = grad_out[0]
    out, smalls, g_scale, g_shift = norm_backward(
        gad, normed[...], inv[...], small, clip, above.astype(F32), tokens[0], shifts
    )
    gin[0] = jnp.where(sec[0] == 0, out, above)
    away[0] = jnp.where(sec[0] == 0, above, out)
    sums[TAPS : TAPS + 8] += smalls
    sums[pl.ds(SCALE + clip, 1)] = g_scale
    sums[pl.ds(SHIFT + clip, 1)] = g_shift

    @pl.when(clip == pl.num_programs(0) - 1)
    def _():
        own[...] = pick(sec[0] == 0, sums[...], sums1[...])
        send[...] = pick(sec[0] == 0, sums1[...], sums[...])


def pick(first, a, b):
    return jnp.where(first, a, b)


def bit_of(spot, step):
    low, high = ORDERS[0][step], ORDERS[1][step]
    return (spot[1] >> (low if low == high else pick(spot[0] == 0, low, high))) & 1


GATHER = (3, 2, 0, 1)


def gather_bit(spot, hop):
    return (spot[1] >> GATHER[hop]) & 1


def gather_slot(spot):
    slot = 0
    for hop in range(len(GATHER)):
        slot = slot + gather_bit(spot, hop) * (1 << hop)
    return slot


def fetch(copies, source, first, rows, target, sem):
    copies.append(pltpu.make_async_copy(source.at[pl.ds(first, rows)], target, sem))
    copies[-1].start()


def pack_body(step, share, sec, place, total0, total1, *refs):
    rows = (8 >> step) * share
    first = pl.multiple_of((1 - bit_of((sec[0], place[0]), step)) * rows, 32)
    if step == 1:
        came, (packet, buffer, sems) = refs[:2], refs[2:]
        copies = []
        for b in range(2):
            fetch(copies, came[b], first, rows, buffer.at[b], sems.at[b])
    else:
        came, packet = refs
    for b, total in enumerate((total0, total1)):
        if step == 1:
            copies[b].wait()
            latest = buffer[b]
        else:
            latest = came[pl.ds(b * 2 * rows + first, rows)]
        packet[b * rows : (b + 1) * rows] = (total[pl.ds(first, rows)] + latest.astype(F32)).astype(BF16)


def share_body(share, total0, total1, came, up, down):
    rows = up.shape[0]
    whole = total0[...] + came[:share].astype(F32)
    for j in range(3):
        up[:, j * TILE : (j + 1) * TILE] = whole[j * rows : (j + 1) * rows]
    down[...] = total1[...] + came[share : 2 * share].astype(F32)


def begin_rows_body(sec, place, speaker, own_sums, got_sums, packet, smalls, held, sems):
    spot = (sec[0], place[0])
    first = spot[0] == 0
    copies = []
    for n, source in enumerate((own_sums, got_sums)):
        fetch(copies, source, 0, SMALL, held.at[n], sems.at[n])
    for copy in copies:
        copy.wait()
    own, other = held[0], held[1]
    low = pick(first, own[SCALE:], other[SCALE:])
    high = pick(first, other[SCALE:], own[SCALE:])
    packet[:16] = jnp.concatenate([low, high], axis=0).astype(BF16)
    lane = lax.broadcasted_iota(jnp.int32, (1, own.shape[1]), 1)
    here = (lane >> 4) == gather_slot(spot)
    which = ((lane >> 3) & 1) * 4 + (lane & 3)
    code = jnp.zeros(lane.shape, jnp.int32)
    for c in range(8):
        code = jnp.where(here & (which == c), speaker[c], code)
    smalls[...] = own[:SCALE] + other[:SCALE]
    smalls[13:14] = (code >> 6).astype(F32)
    smalls[14:15] = (code & 63).astype(F32)
    packet[16:32] = smalls[...].astype(BF16)


def more_rows_body(hop, place, before, after, smalls_in, packet, smalls):
    size = 16 << (hop - 1)
    bit = gather_bit((0, place[0]), hop - 1)
    for source, side in ((before, bit), (after, 1 - bit)):
        packet[pl.ds(pl.multiple_of(side * size, 16), size)] = source[:size]
    smalls[...] = smalls_in[...] + after[size:].astype(F32)
    packet[2 * size :] = smalls[...].astype(BF16)


def tables_body(place, before, after, smalls_in, scale, shift, taps, conv, upb, downb, gain, rows_of):
    size = rows_of.shape[0] // 2
    bit = gather_bit((0, place[0]), len(GATHER) - 1)
    for source, side in ((before, bit), (after, 1 - bit)):
        rows_of[pl.ds(pl.multiple_of(side * size, 16), size)] = source[:size]
    total = smalls_in[...] + after[size:].astype(F32)
    owned = scale.shape[0]
    count = 2 * size
    who = total[13:14, :count] * 64.0 + total[14:15, :count]
    wanted = lax.broadcasted_iota(jnp.int32, (owned, count), 0) + place[0] * owned
    hit = who == wanted.astype(F32)
    kind = (lax.broadcasted_iota(jnp.int32, (owned, count), 1) >> 2) & 1
    for k, out in enumerate((scale, shift)):
        out[...] = dot(jnp.where(hit & (kind == k), 1.0, 0.0).astype(BF16), rows_of[...], NN)
    lanes = total.shape[1] // BLOCKS
    turn = lax.rem(BLOCKS - place[0], BLOCKS)
    cut = pltpu.roll(total, turn * lanes, 1)[:, :lanes]
    for k in range(7):
        taps[k] = cut[k : k + 1]
    conv[...] = cut[CONV : CONV + 1]
    downb[...] = cut[DOWNB : DOWNB + 1]
    gain[...] = cut[GAIN : GAIN + 1]
    line = jnp.concatenate([total[UPB + k : UPB + k + 1] for k in range(3)], axis=1)
    upb[...] = pltpu.roll(line, turn * 3 * lanes, 1)[:, : 3 * lanes]


def struct(shape, dtype):
    return jax.ShapeDtypeStruct(shape, dtype)


def params(limit=None):
    return pltpu.CompilerParams(vmem_limit_bytes=limit * 1024 * 1024 if limit else ALL_VMEM)


def cost(flops, moved):
    return pl.CostEstimate(flops=int(flops), bytes_accessed=int(moved), transcendentals=0)


def local(
    tokens, out_cotangent, speaker, valid, conv_weight, conv_bias, scale_table, shift_table,
    up_weight, up_bias, down_weight, down_bias, layer_scale,
):
    section = lax.axis_index("section").astype(jnp.int32)
    place = lax.axis_index("dp").astype(jnp.int32)
    devices = lax.axis_size("dp")
    clips, frames, width = tokens.shape
    hidden = up_weight.shape[2]
    table_rows = scale_table.shape[1]
    half = clips // 2
    rows = half * frames
    sec = section[None]
    swap = [(0, 1), (1, 0)]

    own_small, other_small = pl.pallas_call(
        prep_body,
        out_shape=[struct((SMALL, width), F32)] * 2,
        in_specs=[SMEM, SMEM] + [VMEM] * 5 + [ANY] * 2,
        out_specs=[VMEM] * 2,
        scratch_shapes=[pltpu.SemaphoreType.DMA((2, 2, half))],
        compiler_params=params(),
        name="prep",
    )(
        sec, speaker, conv_weight.transpose(1, 0, 2), conv_bias, up_bias, down_bias, layer_scale,
        scale_table, shift_table,
    )
    got_small = lax.ppermute(other_small, "section", swap)
    up_own, down_own = up_weight[0], down_weight[0]
    up_got = lax.ppermute(up_own, "section", swap)
    down_got = lax.ppermute(down_own, "section", swap)
    clip_block = (1, frames, width)
    whole_small = pl.BlockSpec((SMALL, width), lambda c, sec: (0, 0))
    half_struct = struct((half, frames, width), BF16)
    whole_struct = struct((clips, frames, width), BF16)
    small_struct = struct((SMALL, width), F32)
    flat_struct = struct((rows, width), BF16)
    tiles = hidden // TILE
    tiled = (tiles, rows, TILE)
    share = hidden // BLOCKS
    gradient = (BLOCKS, share, width)
    gradient_struct = struct(gradient, BF16)
    piece_struct = struct((BLOCKS // 2, share, width), BF16)
    product = 2 * rows * width * hidden

    (
        sums0, sums1, gin1, normed0, inv0, out_own, out_send, gpre0, up_keep,
        down_keep, up_pass, down_pass, up_stay, down_stay, small0,
    ) = pl.pallas_call(
        main_body,
        out_shape=[
            small_struct, small_struct, half_struct, flat_struct, struct((rows, 128), F32),
            whole_struct, half_struct, struct(tiled, BF16), gradient_struct, gradient_struct,
            piece_struct, piece_struct, piece_struct, piece_struct, small_struct,
        ],
        in_specs=[SMEM, SMEM, SMEM, VMEM, VMEM, HBM, HBM, HBM, ANY, HBM, ANY],
        out_specs=[VMEM, VMEM] + [HBM] * 12 + [VMEM],
        scratch_shapes=[
            pltpu.VMEM((width, hidden), BF16),
            pltpu.VMEM((hidden, width), BF16),
            pltpu.VMEM((width, hidden), BF16),
            pltpu.VMEM((hidden, width), BF16),
            pltpu.VMEM(tiled, BF16),
            pltpu.VMEM(tiled, BF16),
            pltpu.VMEM(tiled, BF16),
            pltpu.VMEM(tiled, BF16),
            pltpu.VMEM((rows, width), F32),
            pltpu.VMEM((rows, width), BF16),
            pltpu.VMEM((rows, width), BF16),
            pltpu.VMEM((rows, 128), F32),
            pltpu.VMEM((rows, width), BF16),
            pltpu.VMEM((rows, width), F32),
            pltpu.VMEM((rows, width), BF16),
            pltpu.VMEM((half, frames, width), BF16),
            pltpu.VMEM((half, frames, width), BF16),
            pltpu.VMEM((half, frames, width), BF16),
            pltpu.VMEM((half, frames, width), BF16),
            pltpu.VMEM((SMALL, width), F32),
            pltpu.VMEM((SMALL, width), F32),
            pltpu.VMEM((len(OFFSETS) * frames, frames), BF16),
            pltpu.VMEM(gradient, BF16),
            pltpu.VMEM(gradient, BF16),
            pltpu.VMEM(gradient, BF16),
            pltpu.VMEM(gradient, BF16),
            pltpu.SemaphoreType.DMA((9, 2)),
            pltpu.SemaphoreType.DMA((half,)),
            pltpu.SemaphoreType.DMA((2, 2, 2)),
        ],
        compiler_params=params(),
        cost_estimate=cost(11 * product, 24 << 20),
        name="main",
    )(
        sec, place[None], valid, own_small, got_small, tokens, out_cotangent, up_own, up_got, down_own, down_got
    )
    swapped = []
    for piece in (up_pass, down_pass, up_stay, down_stay):
        swapped.append(lax.ppermute(piece, "section", swap))
    pairs = [[up_keep, swapped[0], swapped[2]], [down_keep, swapped[1], swapped[3]]]
    got_out = lax.ppermute(out_send, "section", swap)

    gin_own, gin_send, own_sums, sums_send = pl.pallas_call(
        last_body,
        grid_spec=pltpu.PrefetchScalarGridSpec(
            num_scalar_prefetch=1,
            grid=(half,),
            in_specs=[
                pl.BlockSpec((tiles, frames, TILE), lambda c, sec: (0, c, 0)),
                HBM,
                ANY,
                pl.BlockSpec((frames, width), lambda c, sec: (c, 0)),
                pl.BlockSpec((frames, 128), lambda c, sec: (c, 0)),
                whole_small,
                pl.BlockSpec(clip_block, lambda c, sec: (c, 0, 0)),
                pl.BlockSpec(clip_block, lambda c, sec: (sec[0] * half + c, 0, 0)),
                whole_small,
                whole_small,
            ],
            out_specs=[
                pl.BlockSpec(clip_block, lambda c, sec: (sec[0] * half + c, 0, 0)),
                pl.BlockSpec(clip_block, lambda c, sec: (c, 0, 0)),
                whole_small,
                whole_small,
            ],
            scratch_shapes=[
                pltpu.VMEM((width, hidden), BF16),
                pltpu.VMEM((len(OFFSETS) * frames, frames), BF16),
                pltpu.VMEM((SMALL, width), F32),
                pltpu.SemaphoreType.DMA,
            ],
        ),
        out_shape=[whole_struct, half_struct, small_struct, small_struct],
        compiler_params=params(),
        cost_estimate=cost(2 * half * product, 12 << 20),
        name="last",
    )(sec, gpre0, up_own, up_got, normed0, inv0, small0, gin1, tokens, sums0, sums1)
    got_gin = lax.ppermute(gin_send, "section", swap)
    got_sums = lax.ppermute(sums_send, "section", swap)

    def joined(whole, got):
        return lax.dynamic_update_slice(whole, got, ((1 - section) * half, 0, 0))[None]

    block_outputs = joined(out_own, got_out)
    input_grads = joined(gin_own, got_gin)
    if devices == BLOCKS:
        outs = halved(sec, place[None], speaker, pairs, own_sums, got_sums, table_rows)
    else:
        outs = scattered(section, place, devices, speaker, pairs, own_sums, got_sums, table_rows)
    return (block_outputs, input_grads) + outs


def exchanged(packet, step):
    devices = lax.axis_size("dp")
    moves = [
        (s * devices + i, s * devices + (i ^ (1 << ORDERS[s][step])))
        for s in range(2)
        for i in range(devices)
    ]
    return lax.ppermute(packet, PAIR, moves)


def halved(sec, place, speaker, pairs, own_sums, got_sums, table_rows):
    _, share, width = pairs[0][0].shape
    pairs = [[piece.reshape(-1, width) for piece in pair] for pair in pairs]
    spot = (sec[0], place[0])
    half_rows = 8 * share

    def part(array, first, count):
        return lax.dynamic_slice_in_dim(array, first, count, 0).astype(F32)

    bit = bit_of(spot, 0)
    latest, totals = [None, None], [None, None]
    for b in (0, 1):
        keep, passed, stays = pairs[b]
        own = lax.optimization_barrier(part(keep, (1 - bit) * half_rows, half_rows))
        packet = (own + passed.astype(F32)).astype(BF16)
        latest[b] = exchanged(packet, 0)
        keep, stays, _ = lax.optimization_barrier((keep, stays, own_sums))
        totals[b] = part(keep, bit * half_rows, half_rows) + stays.astype(F32)

    def small_call(body, outs, scalars, operands, scratch=(), specs=None, limit=8):
        return pl.pallas_call(
            body,
            out_shape=outs,
            in_specs=[SMEM] * len(scalars) + (specs or [VMEM] * len(operands)),
            out_specs=[VMEM] * len(outs),
            scratch_shapes=scratch,
            compiler_params=params(limit),
            cost_estimate=cost(0, 2 << 20),
        )(*scalars, *operands)

    def row_outs(hop):
        return [struct(((16 << hop) + 16, width), BF16), struct((SCALE, width), F32)]

    rows_packet, smalls = small_call(
        begin_rows_body, row_outs(0), [sec, place, speaker],
        [own_sums, got_sums],
        [pltpu.VMEM((2, SMALL, width), F32), pltpu.SemaphoreType.DMA((2,))], [HBM] * 2,
    )
    for hop in range(len(GATHER)):
        more = lax.ppermute(
            rows_packet, "dp", [(i, i ^ (1 << GATHER[hop])) for i in range(BLOCKS)]
        )
        operands = [rows_packet, more, smalls]
        if hop + 1 < len(GATHER):
            rows_packet, smalls = small_call(
                functools.partial(more_rows_body, hop + 1), row_outs(hop + 1), [place],
                operands,
            )
    owned = table_rows // BLOCKS
    lanes = width // BLOCKS
    one = struct((1, lanes), F32)
    scale, shift, taps, conv, upb, downb, gain = small_call(
        tables_body,
        [
            struct((owned, width), F32),
            struct((owned, width), F32),
            struct((7, 1, lanes), F32),
            one,
            struct((1, 3 * lanes), F32),
            one,
            one,
        ],
        [place],
        operands,
        [pltpu.VMEM((16 * BLOCKS, width), BF16)],
    )

    for step in range(1, 4):
        rows = (8 >> step) * share
        first = bit_of(spot, step) * rows
        packet_struct = [struct((2 * rows, width), BF16)]
        if step == 1:
            (packet,) = small_call(
                functools.partial(pack_body, step, share), packet_struct, [sec, place],
                totals + latest,
                [pltpu.VMEM((2, rows, width), BF16), pltpu.SemaphoreType.DMA((2,))],
                [VMEM] * 2 + [ANY] * 2,
            )
        else:
            (packet,) = small_call(
                functools.partial(pack_body, step, share), packet_struct, [sec, place],
                totals + latest[:1],
            )
        got = exchanged(packet, step)
        bases = (0, 0) if step == 1 else (0, 2 * rows)
        totals = [
            part(totals[b], first, rows) + part(latest[b], bases[b] + first, rows) for b in range(2)
        ]
        latest = [got, got]
    up, down = small_call(
        functools.partial(share_body, share),
        [struct((width // BLOCKS, 3 * TILE), F32), struct((share, width), F32)],
        [],
        totals + latest[:1],
    )
    return (
        taps.transpose(1, 0, 2), conv, scale[None], shift[None], up[None], upb, down[None], downb, gain
    )


def scattered(section, place, devices, speaker, pairs, own_sums, got_sums, table_rows):
    first_section = section == 0
    smalls = lax.psum(own_sums[:SCALE] + got_sums[:SCALE], "dp")
    clip_rows = jnp.stack([own_sums[SCALE:], got_sums[SCALE:]])
    clip_rows = pick(first_section, clip_rows, clip_rows[::-1]).astype(BF16)
    clips = speaker.shape[0]
    width = clip_rows.shape[-1]
    clip_rows = clip_rows.reshape(2, 2, clips // 2, width).transpose(1, 0, 2, 3).reshape(2, clips, width)
    gathered = lax.all_gather(clip_rows, "dp", axis=1, tiled=True)
    who = lax.all_gather(speaker, "dp", tiled=True)
    owned = table_rows // devices
    wanted = place * owned + jnp.arange(owned, dtype=jnp.int32)
    chosen = (who[None, :] == wanted[:, None]).astype(BF16)
    tables = [jnp.dot(chosen, gathered[k], preferred_element_type=F32) for k in range(2)]
    low, high = ORDERS[0][0], ORDERS[1][0]
    leaves = 1 - ((place >> pick(first_section, low, high)) & 1)
    natural = []
    for keep, gone, stay in pairs:
        other = pick(leaves == 0, jnp.concatenate([gone, stay]), jnp.concatenate([stay, gone]))
        whole = keep.astype(F32) + other.astype(F32)
        both = [jnp.stack([whole[position(i, order)] for i in range(BLOCKS)]) for order in ORDERS]
        natural.append(pick(first_section, both[0], both[1]))
    _, rows, width = natural[0].shape
    tiles = rows * BLOCKS // TILE
    up = natural[0].reshape(BLOCKS, tiles, rows // tiles, TILE).transpose(0, 2, 1, 3)
    up_share = lax.psum_scatter(up.reshape(width, -1), "dp", scatter_dimension=0, tiled=True)
    down_share = lax.psum_scatter(natural[1].reshape(-1, width), "dp", scatter_dimension=0, tiled=True)
    lanes = width // devices
    own_lanes = lax.dynamic_slice_in_dim(smalls, place * lanes, lanes, 1)
    upb = lax.dynamic_slice_in_dim(smalls[UPB : UPB + 3].reshape(-1), place * 3 * lanes, 3 * lanes, 0)
    return (
        own_lanes[TAPS : TAPS + 7][None],
        own_lanes[CONV : CONV + 1],
        tables[0][None],
        tables[1][None],
        up_share[None],
        upb[None],
        down_share[None],
        own_lanes[DOWNB : DOWNB + 1],
        own_lanes[GAIN : GAIN + 1],
    )


def solution(mesh):
    placed = (
        P("dp", None, None),
        P("dp", None, None),
        P("dp"),
        P("dp"),
        P("section", None, None),
        P("section", None),
        P("section", None, None),
        P("section", None, None),
        P("section", None, None),
        P("section", None),
        P("section", None, None),
        P("section", None),
        P("section", None),
    )

    return jax.shard_map(
        local,
        mesh=mesh,
        in_specs=placed,
        out_specs=(
            P("section", "dp", None, None),
            P("section", "dp", None, None),
            P("section", None, "dp"),
            P("section", "dp"),
            P("section", "dp", None),
            P("section", "dp", None),
            P("section", "dp", None),
            P("section", "dp"),
            P("section", "dp", None),
            P("section", "dp"),
            P("section", "dp"),
        ),
        check_vma=False,
    )
```

profile of v0, /device:TPU:0, one launch (start us, length us, event | category | flops | bytes accessed | tf_op | source)
XLA Modules:
  0.0 119.0 jit_solution(17626948060613733206)
XLA Ops:
  0.6 0.6 collective-permute-start.1
  1.2 0.1 collective-permute-start.2
  1.3 2.4 %prep.1 = (f32[24,512]{1,0:T(8,128)}, f32[24,512]{1,0:T(8,128)}) custom-call(s32[1]{0:T(128)} %bitcast.sec, s32[8]{0:T(128)} %speaker.3, f32[7,1,512]{2,1,0:T(1,128)} %bitcast.30, f32[1,512]{1,0:T(1,128)} %conv.1, f32[1,1536]{1,0:T(1,128)} %upb.1, f32[1,512]{1,0:T(1,128)} %downb.1, f32[1,512]{1,0:T(1,128)} %gain.1, f32[1,2560,512]{2,1,0:T(8,128)} %scale_hbm.1, ...), custom_call_target="tpu_custom_call" | custom-call | tf_op jit(solution)/shard_map/prep/pallas_call | solution.py:562
  3.7 0.5 collective-permute-start
  4.2 2.7 %collective-permute-done.got_small = f32[24,512]{1,0:T(8,128)} collective-permute-done((f32[24,512]{1,0:T(8,128)}, f32[24,512]{1,0:T(8,128)}, u32[]{:S(2)}, u32[]{:S(2)}) %collective-permute-start) | collective-permute-done | bytes 49184 | tf_op jit(solution)/shard_map/ppermute | solution.py:574
  6.9 35.2 %main.1 = (f32[24,512]{1,0:T(8,128)}, f32[24,512]{1,0:T(8,128)}, bf16[4,256,512]{2,1,0:T(8,128)(2,1)}, bf16[1024,512]{1,0:T(8,128)(2,1)}, f32[1024,128]{1,0:T(8,...) custom-call(s32[1]{0:T(128)} %bitcast.sec, ...), custom_call_target="tpu_custom_call" | custom-call | flops 17716740096 | bytes 25165824 | tf_op jit(solution)/shard_map/main/pallas_call | solution.py:595
  42.1 0.0 copy-start.2
  42.1 0.4 collective-permute-start.14
  42.5 0.2 collective-permute-start.11
  42.7 0.3 collective-permute-start.3
  43.0 0.2 collective-permute-start.13
  43.2 0.3 collective-permute-start.10
  43.5 1.3 %dynamic-slice_convert_fusion = f32[768,512]{1,0:T(8,128)S(1)} fusion(bf16[1536,512]{1,0:T(8,128)(2,1)} %bitcast.28, s32[]{:T(128)S(6)} %select_n.53), kind=kLoop, calls=%fused_computation.9 | loop fusion | flops 393216 | bytes 2359300 | tf_op jit(solution)/shard_map/convert_element_type | solution.py:714
  44.9 0.2 dynamic-slice_convert_fusion.1
  45.1 1.3 %fusion = bf16[768,512]{1,0:T(8,128)(2,1)} fusion(f32[768,512]{1,0:T(8,128)S(1)} %dynamic-slice_convert_fusion, bf16[8,96,512]{2,1,0:T(8,128)(2,1)S(1)} %collective-permute-done.14), kind=kLoop, calls=%fused_computation.1 | loop fusion | flops 1179648 | bytes 3145728 | tf_op jit(solution)/shard_map/convert_element_type | solution.py:721
  46.4 2.6 %collective-permute-start.15 = (bf16[768,512]{1,0:T(8,128)(2,1)}, bf16[768,512]{1,0:T(8,128)(2,1)}, u32[]{:S(2)}, u32[]{:S(2)}) collective-permute-start(bf16[768,512]{1,0:T(8,128)(2,1)} %fusion), channel_id=1, source_target_pairs={{0,1},{1,0},{2,3},{3,2},{4,5},{5,4},{6,7},{7,6},{8,9},{9,8},{10,11... | collective-permute-start | bytes 2359304 | tf_op jit(solution)/shard_map/ppermute | solution.py:704
  49.0 1.3 %fusion.1 = bf16[768,512]{1,0:T(8,128)(2,1)} fusion(f32[768,512]{1,0:T(8,128)S(1)} %dynamic-slice_convert_fusion.1, bf16[8,96,512]{2,1,0:T(8,128)(2,1)S(1)} %collective-permute-done.11), kind=kLoop, calls=%fused_computation.3 | loop fusion | flops 1179648 | bytes 3145728 | tf_op jit(solution)/shard_map/convert_element_type | solution.py:721
  50.2 9.9 %last.1 = (bf16[8,256,512]{2,1,0:T(8,128)(2,1)}, bf16[4,256,512]{2,1,0:T(8,128)(2,1)}, f32[24,512]{1,0:T(8,128)}, f32[24,512]{1,0:T(8,128)}) custom-call(s32[1]{0:T(128)} %bitcast.sec, bf16[3,1024,512]{2,1,0:T(8,128)(2,1)} %get-tuple-element.57.gpre, bf16[512,1536]{1,0:T(8,128)(2,1)} %bitcast.37, bf16[512,1536]{1,0:T(8,128)(2,1)} %collective-permute-done.1.up_got, ...), custom_call_target="tpu_custom_call" | custom-call | flops 12884901888 | bytes 12582912 | tf_op jit(solution)/shard_map/last/pallas_call | solution.py:647
  60.2 2.3 %convert_add_fusion.2 = (f32[768,512]{1,0:T(8,128)S(1)}, f32[768,512]{1,0:T(8,128)S(1)}) fusion(bf16[768,512]{1,0:T(8,128)(2,1)} %bitcast.16, bf16[1536,512]{1,0:T(8,128)(2,1)} %bitcast.29, s32[]{:T(128)S(6)} %select_n.50, bf16[768,512]{1,0:T(8,128)(2,1)} %bitcast.13, bf16[1536,512]{1,0:T(8,128)(2,1)} %bitcast.26), kind=kLoop, calls=%fused_computation.4 | loop fusion | flops 2359296 | bytes 6291460 | tf_op jit(solution)/shard_map/add | solution.py:724
  62.6 5.1 %collective-permute-done.12.refs_0_ = bf16[768,512]{1,0:T(8,128)(2,1)} collective-permute-done((bf16[768,512]{1,0:T(8,128)(2,1)}, bf16[768,512]{1,0:T(8,128)(2,1)}, u32[]{:S(2)}, u32[]{:S(2)}) %collective-permute-start.12) | collective-permute-done | bytes 786464 | tf_op jit(solution)/shard_map/ppermute | solution.py:704
  67.7 2.1 %shard_map.217 = bf16[768,512]{1,0:T(8,128)(2,1)} custom-call(s32[1]{0:T(128)} %bitcast.sec, s32[1]{0:T(128)} %bitcast.1.place, f32[768,512]{1,0:T(8,128)S(1)} %get-tuple-element.100.total0, f32[768,512]{1,0:T(8,128)S(1)} %get-tuple-element.99.total1, bf16[768,512]{1,0:T(8,128)(2,1)} %collective-permute-done.12.refs_0_, ...), custom_call_target="tpu_custom_call" | custom-call | bytes 2097152 | tf_op jit(solution)/shard_map/pallas_call | solution.py:727
  69.8 2.1 %collective-permute-start.16 = (bf16[768,512]{1,0:T(8,128)(2,1)}, bf16[768,512]{1,0:T(8,128)(2,1)}, u32[]{:S(2)}, u32[]{:S(2)}) collective-permute-start(bf16[768,512]{1,0:T(8,128)(2,1)} %shard_map.217), channel_id=1, source_target_pairs={{0,2},{1,3},{2,0},{3,1},{4,6},{5,7},{6,4},{7,5},{8,10},{9,11},{10,... | collective-permute-start | bytes 2359304 | tf_op jit(solution)/shard_map/ppermute | solution.py:704
  71.9 0.5 collective-permute-start.5
  72.4 2.5 %collective-permute-done.5.got_sums = f32[24,512]{1,0:T(8,128)S(1)} collective-permute-done((f32[24,512]{1,0:T(8,128)S(1)}, f32[24,512]{1,0:T(8,128)S(1)}, u32[]{:S(2)}, u32[]{:S(2)}) %collective-permute-start.5) | collective-permute-done | bytes 49184 | tf_op jit(solution)/shard_map/ppermute | solution.py:683
  74.9 0.7 shard_map.212
  75.6 2.6 %collective-permute-start.6 = (bf16[32,512]{1,0:T(8,128)(2,1)S(1)}, bf16[32,512]{1,0:T(8,128)(2,1)S(1)}, u32[]{:S(2)}, u32[]{:S(2)}) collective-permute-start(bf16[32,512]{1,0:T(8,128)(2,1)S(1)} %get-tuple-element.68.before), channel_id=1, source_target_pairs={{0,8},{1,9},{2,10},{3,11},{4,12},{5,13},{6,14},{7,15},{8,0},{9,1},... | collective-permute-start | bytes 98312 | tf_op jit(solution)/shard_map/ppermute | solution.py:746
  78.3 2.6 %collective-permute-done.6.after = bf16[32,512]{1,0:T(8,128)(2,1)S(1)} collective-permute-done((bf16[32,512]{1,0:T(8,128)(2,1)S(1)}, bf16[32,512]{1,0:T(8,128)(2,1)S(1)}, u32[]{:S(2)}, u32[]{:S(2)}) %collective-permute-start.6) | collective-permute-done | bytes 32800 | tf_op jit(solution)/shard_map/ppermute | solution.py:746
  80.9 1.3 %collective-permute-start.7 = (bf16[48,512]{1,0:T(8,128)(2,1)S(1)}, bf16[48,512]{1,0:T(8,128)(2,1)S(1)}, u32[]{:S(2)}, u32[]{:S(2)}) collective-permute-start(bf16[48,512]{1,0:T(8,128)(2,1)S(1)} %get-tuple-element.70.before), channel_id=1, source_target_pairs={{0,4},{1,5},{2,6},{3,7},{4,0},{5,1},{6,2},{7,3},{8,12},{9,13},{10,... | collective-permute-start | bytes 147464 | tf_op jit(solution)/shard_map/ppermute | solution.py:746
  82.2 2.9 %collective-permute-done.7.after = bf16[48,512]{1,0:T(8,128)(2,1)S(1)} collective-permute-done((bf16[48,512]{1,0:T(8,128)(2,1)S(1)}, bf16[48,512]{1,0:T(8,128)(2,1)S(1)}, u32[]{:S(2)}, u32[]{:S(2)}) %collective-permute-start.7) | collective-permute-done | bytes 49184 | tf_op jit(solution)/shard_map/ppermute | solution.py:746
  85.0 1.6 %collective-permute-start.8 = (bf16[80,512]{1,0:T(8,128)(2,1)S(1)}, bf16[80,512]{1,0:T(8,128)(2,1)S(1)}, u32[]{:S(2)}, u32[]{:S(2)}) collective-permute-start(bf16[80,512]{1,0:T(8,128)(2,1)S(1)} %get-tuple-element.72.before), channel_id=1, source_target_pairs={{0,1},{1,0},{2,3},{3,2},{4,5},{5,4},{6,7},{7,6},{8,9},{9,8},{10,11... | collective-permute-start | bytes 245768 | tf_op jit(solution)/shard_map/ppermute | solution.py:746
  86.6 2.9 %collective-permute-done.8.after = bf16[80,512]{1,0:T(8,128)(2,1)S(1)} collective-permute-done((bf16[80,512]{1,0:T(8,128)(2,1)S(1)}, bf16[80,512]{1,0:T(8,128)(2,1)S(1)}, u32[]{:S(2)}, u32[]{:S(2)}) %collective-permute-start.8) | collective-permute-done | bytes 81952 | tf_op jit(solution)/shard_map/ppermute | solution.py:746
  89.6 0.1 collective-permute-start.9
  89.7 5.1 %collective-permute-done.9.after = bf16[144,512]{1,0:T(8,128)(2,1)S(1)} collective-permute-done((bf16[144,512]{1,0:T(8,128)(2,1)S(1)}, bf16[144,512]{1,0:T(8,128)(2,1)S(1)}, u32[]{:S(2)}, u32[]{:S(2)}) %collective-permute-start.9) | collective-permute-done | bytes 147488 | tf_op jit(solution)/shard_map/ppermute | solution.py:746
  94.8 1.1 shard_map.216
  95.8 1.1 convert_add_fusion.4.total1
  97.0 1.1 convert_add_fusion.5.total0
  98.1 0.0 copy-start.3
  98.1 1.3 %shard_map.218 = bf16[384,512]{1,0:T(8,128)(2,1)S(1)} custom-call(s32[1]{0:T(128)} %bitcast.sec, s32[1]{0:T(128)} %bitcast.1.place, f32[384,512]{1,0:T(8,128)S(1)} %convert_add_fusion.5.total0, f32[384,512]{1,0:T(8,128)S(1)} %convert_add_fusion.4.total1, bf16[768,512]{1,0:T(8,128)(2,1)} %collective-permute-done.16.refs_0_), custom_call_target="tpu_custom_call" | custom-call | bytes 2097152 | tf_op jit(solution)/shard_map/pallas_call | solution.py:727
  99.4 1.3 %collective-permute-start.17 = (bf16[384,512]{1,0:T(8,128)(2,1)S(1)}, bf16[384,512]{1,0:T(8,128)(2,1)S(1)}, u32[]{:S(2)}, u32[]{:S(2)}) collective-permute-start(bf16[384,512]{1,0:T(8,128)(2,1)S(1)} %shard_map.218), channel_id=1, source_target_pairs={{0,4},{1,5},{2,6},{3,7},{4,0},{5,1},{6,2},{7,3},{8,12},{9,13},{10,... | collective-permute-start | bytes 1179656 | tf_op jit(solution)/shard_map/ppermute | solution.py:704
  100.7 1.3 %bitcast_dynamic-update-slice_fusion.1 = bf16[1,8,256,512]{3,2,1,0:T(8,128)(2,1)S(1)} fusion(bf16[1,8,256,512]{3,2,1,0:T(8,128)(2,1)S(1)} %bitcast.31, s32[]{:T(128)S(6)} %select_n.48, bf16[4,256,512]{2,1,0:T(8,128)(2,1)} %collective-permute-done.3), kind=kLoop, calls=%fused_computation.7 | loop fusion | bytes 2097156 | tf_op jit(solution)/shard_map/dynamic_update_slice | solution.py:686
  102.1 0.0 copy-start.4
  102.1 1.7 %convert_add_fusion.6 = (f32[192,512]{1,0:T(8,128)S(1)}, f32[192,512]{1,0:T(8,128)S(1)}) fusion(f32[384,512]{1,0:T(8,128)S(1)} %convert_add_fusion.4.total1, s32[]{:T(128)S(6)} %select_n.55, bf16[768,512]{1,0:T(8,128)(2,1)} %collective-permute-done.16.refs_0_, s32[]{:T(128)S(6)} %select_n.59, s32[]{:T(128)S(6)} %select_n.56, ...), kind=kLoop, calls=%fused_computation.12 | loop fusion | flops 393216 | bytes 1966092 | tf_op jit(solution)/shard_map/add | solution.py:793
  103.8 5.5 %collective-permute-done.17.refs_0_ = bf16[384,512]{1,0:T(8,128)(2,1)S(1)} collective-permute-done((bf16[384,512]{1,0:T(8,128)(2,1)S(1)}, bf16[384,512]{1,0:T(8,128)(2,1)S(1)}, u32[]{:S(2)}, u32[]{:S(2)}) %collective-permute-start.17) | collective-permute-done | bytes 393248 | tf_op jit(solution)/shard_map/ppermute | solution.py:704
  109.4 2.3 %collective-permute-start.18 = (bf16[192,512]{1,0:T(8,128)(2,1)S(1)}, bf16[192,512]{1,0:T(8,128)(2,1)S(1)}, u32[]{:S(2)}, u32[]{:S(2)}) collective-permute-start(bf16[192,512]{1,0:T(8,128)(2,1)S(1)} %shard_map.219), channel_id=1, source_target_pairs={{0,8},{1,9},{2,10},{3,11},{4,12},{5,13},{6,14},{7,15},{8,0},{9,1},... | collective-permute-start | bytes 589832 | tf_op jit(solution)/shard_map/ppermute | solution.py:704
  111.8 1.3 %bitcast_dynamic-update-slice_fusion = bf16[1,8,256,512]{3,2,1,0:T(8,128)(2,1)S(1)} fusion(bf16[1,8,256,512]{3,2,1,0:T(8,128)(2,1)S(1)} %bitcast.32, s32[]{:T(128)S(6)} %select_n.48, bf16[4,256,512]{2,1,0:T(8,128)(2,1)} %collective-permute-done.4), kind=kLoop, calls=%fused_computation.6 | loop fusion | bytes 2097156 | tf_op jit(solution)/shard_map/dynamic_update_slice | solution.py:686
  113.1 0.1 convert_add_fusion.8
  113.2 5.0 %collective-permute-done.18.came = bf16[192,512]{1,0:T(8,128)(2,1)S(1)} collective-permute-done((bf16[192,512]{1,0:T(8,128)(2,1)S(1)}, bf16[192,512]{1,0:T(8,128)(2,1)S(1)}, u32[]{:S(2)}, u32[]{:S(2)}) %collective-permute-start.18) | collective-permute-done | bytes 196640 | tf_op jit(solution)/shard_map/ppermute | solution.py:704
  118.2 0.8 shard_map.220
  (29 shorter events, 0.1 us)
Async XLA Ops:
  0.6 6.3 %collective-permute-start.1 = (bf16[512,1536]{1,0:T(8,128)(2,1)}, bf16[512,1536]{1,0:T(8,128)(2,1)}, u32[]{:S(2)}, u32[]{:S(2)}) collective-permute-start(bf16[512,1536]{1,0:T(8,128)(2,1)} %bitcast.35), channel_id=1, source_target_pairs={{0,16},{16,0},{1,17},{17,1},{2,18},{18,2},{3,19},{19,3},{4,20},{20... | collective-permute-start | bytes 4718600 | tf_op jit(solution)/shard_map/ppermute | solution.py:576
  1.2 5.7 %collective-permute-start.2 = (bf16[1536,512]{1,0:T(8,128)(2,1)}, bf16[1536,512]{1,0:T(8,128)(2,1)}, u32[]{:S(2)}, u32[]{:S(2)}) collective-permute-start(bf16[1536,512]{1,0:T(8,128)(2,1)} %bitcast.33), channel_id=1, source_target_pairs={{0,16},{16,0},{1,17},{17,1},{2,18},{18,2},{3,19},{19,3},{4,20},{20... | collective-permute-start | bytes 4718600 | tf_op jit(solution)/shard_map/ppermute | solution.py:577
  3.7 3.2 %collective-permute-start = (f32[24,512]{1,0:T(8,128)}, f32[24,512]{1,0:T(8,128)}, u32[]{:S(2)}, u32[]{:S(2)}) collective-permute-start(f32[24,512]{1,0:T(8,128)} %get-tuple-element.54), channel_id=1, source_target_pairs={{0,16},{16,0},{1,17},{17,1},{2,18},{18,2},{3,19},{19,3},{4,20},{20... | collective-permute-start | bytes 147464 | tf_op jit(solution)/shard_map/ppermute | solution.py:574
  42.1 2.8 %copy-start.2 = (bf16[16,96,512]{2,1,0:T(8,128)(2,1)S(1)}, bf16[16,96,512]{2,1,0:T(8,128)(2,1)}, u32[]{:S(2)}) copy-start(bf16[16,96,512]{2,1,0:T(8,128)(2,1)} %get-tuple-element.80) | copy-start | bytes 4718596
  42.1 3.0 %collective-permute-start.14 = (bf16[8,96,512]{2,1,0:T(8,128)(2,1)}, bf16[8,96,512]{2,1,0:T(8,128)(2,1)S(1)}, u32[]{:S(2)}, u32[]{:S(2)}) collective-permute-start(bf16[8,96,512]{2,1,0:T(8,128)(2,1)} %get-tuple-element.89), channel_id=1, source_target_pairs={{0,16},{16,0},{1,17},{17,1},{2,18},{18,2},{3,19},{19,3},{4,20},{20... | collective-permute-start | bytes 2359304 | tf_op jit(solution)/shard_map/ppermute | solution.py:643
  42.5 6.5 %collective-permute-start.11 = (bf16[8,96,512]{2,1,0:T(8,128)(2,1)}, bf16[8,96,512]{2,1,0:T(8,128)(2,1)S(1)}, u32[]{:S(2)}, u32[]{:S(2)}) collective-permute-start(bf16[8,96,512]{2,1,0:T(8,128)(2,1)} %get-tuple-element.84), channel_id=1, source_target_pairs={{0,16},{16,0},{1,17},{17,1},{2,18},{18,2},{3,19},{19,3},{4,20},{20... | collective-permute-start | bytes 2359304 | tf_op jit(solution)/shard_map/ppermute | solution.py:643
  42.7 58.1 %collective-permute-start.3 = (bf16[4,256,512]{2,1,0:T(8,128)(2,1)}, bf16[4,256,512]{2,1,0:T(8,128)(2,1)}, u32[]{:S(2)}, u32[]{:S(2)}) collective-permute-start(bf16[4,256,512]{2,1,0:T(8,128)(2,1)} %get-tuple-element.56), channel_id=1, source_target_pairs={{0,16},{16,0},{1,17},{17,1},{2,18},{18,2},{3,19},{19,3},{4,20},{20... | collective-permute-start | bytes 3145736 | tf_op jit(solution)/shard_map/ppermute | solution.py:645
  43.0 17.2 %collective-permute-start.13 = (bf16[8,96,512]{2,1,0:T(8,128)(2,1)}, bf16[8,96,512]{2,1,0:T(8,128)(2,1)}, u32[]{:S(2)}, u32[]{:S(2)}) collective-permute-start(bf16[8,96,512]{2,1,0:T(8,128)(2,1)} %get-tuple-element.86), channel_id=1, source_target_pairs={{0,16},{16,0},{1,17},{17,1},{2,18},{18,2},{3,19},{19,3},{4,20},{20... | collective-permute-start | bytes 2359304 | tf_op jit(solution)/shard_map/ppermute | solution.py:643
  43.2 17.0 %collective-permute-start.10 = (bf16[8,96,512]{2,1,0:T(8,128)(2,1)}, bf16[8,96,512]{2,1,0:T(8,128)(2,1)}, u32[]{:S(2)}, u32[]{:S(2)}) collective-permute-start(bf16[8,96,512]{2,1,0:T(8,128)(2,1)} %get-tuple-element.81), channel_id=1, source_target_pairs={{0,16},{16,0},{1,17},{17,1},{2,18},{18,2},{3,19},{19,3},{4,20},{20... | collective-permute-start | bytes 2359304 | tf_op jit(solution)/shard_map/ppermute | solution.py:643
  46.4 16.2 %collective-permute-start.15 = (bf16[768,512]{1,0:T(8,128)(2,1)}, bf16[768,512]{1,0:T(8,128)(2,1)}, u32[]{:S(2)}, u32[]{:S(2)}) collective-permute-start(bf16[768,512]{1,0:T(8,128)(2,1)} %fusion), channel_id=1, source_target_pairs={{0,1},{1,0},{2,3},{3,2},{4,5},{5,4},{6,7},{7,6},{8,9},{9,8},{10,11... | collective-permute-start | bytes 2359304 | tf_op jit(solution)/shard_map/ppermute | solution.py:704
  50.2 17.4 %collective-permute-start.12 = (bf16[768,512]{1,0:T(8,128)(2,1)}, bf16[768,512]{1,0:T(8,128)(2,1)}, u32[]{:S(2)}, u32[]{:S(2)}) collective-permute-start(bf16[768,512]{1,0:T(8,128)(2,1)} %fusion.1), channel_id=1, source_target_pairs={{0,1},{1,0},{2,3},{3,2},{4,5},{5,4},{6,7},{7,6},{8,9},{9,8},{10,11... | collective-permute-start | bytes 2359304 | tf_op jit(solution)/shard_map/ppermute | solution.py:704
  67.7 4.2 %copy-start.7 = (f32[24,512]{1,0:T(8,128)S(1)}, f32[24,512]{1,0:T(8,128)}, u32[]{:S(2)}) copy-start(f32[24,512]{1,0:T(8,128)} %get-tuple-element.67) | copy-start | bytes 147460
  67.7 7.2 %copy-start = (f32[24,512]{1,0:T(8,128)S(1)}, f32[24,512]{1,0:T(8,128)}, u32[]{:S(2)}) copy-start(f32[24,512]{1,0:T(8,128)} %get-tuple-element.66.own_sums) | copy-start | bytes 147460
  67.7 7.2 %copy-start.1 = (s32[8]{0:T(128)S(1)}, s32[8]{0:T(128)}, u32[]{:S(2)}) copy-start(s32[8]{0:T(128)} %speaker.3) | copy-start | bytes 100
  69.8 28.3 %collective-permute-start.16 = (bf16[768,512]{1,0:T(8,128)(2,1)}, bf16[768,512]{1,0:T(8,128)(2,1)}, u32[]{:S(2)}, u32[]{:S(2)}) collective-permute-start(bf16[768,512]{1,0:T(8,128)(2,1)} %shard_map.217), channel_id=1, source_target_pairs={{0,2},{1,3},{2,0},{3,1},{4,6},{5,7},{6,4},{7,5},{8,10},{9,11},{10,... | collective-permute-start | bytes 2359304 | tf_op jit(solution)/shard_map/ppermute | solution.py:704
  71.9 39.9 %collective-permute-start.4 = (bf16[4,256,512]{2,1,0:T(8,128)(2,1)}, bf16[4,256,512]{2,1,0:T(8,128)(2,1)}, u32[]{:S(2)}, u32[]{:S(2)}) collective-permute-start(bf16[4,256,512]{2,1,0:T(8,128)(2,1)} %get-tuple-element.65), channel_id=1, source_target_pairs={{0,16},{16,0},{1,17},{17,1},{2,18},{18,2},{3,19},{19,3},{4,20},{20... | collective-permute-start | bytes 3145736 | tf_op jit(solution)/shard_map/ppermute | solution.py:682
  71.9 3.0 %collective-permute-start.5 = (f32[24,512]{1,0:T(8,128)S(1)}, f32[24,512]{1,0:T(8,128)S(1)}, u32[]{:S(2)}, u32[]{:S(2)}) collective-permute-start(f32[24,512]{1,0:T(8,128)S(1)} %copy-done.7), channel_id=1, source_target_pairs={{0,16},{16,0},{1,17},{17,1},{2,18},{18,2},{3,19},{19,3},{4,20},{20... | collective-permute-start | bytes 147464 | tf_op jit(solution)/shard_map/ppermute | solution.py:683
  75.6 5.2 %collective-permute-start.6 = (bf16[32,512]{1,0:T(8,128)(2,1)S(1)}, bf16[32,512]{1,0:T(8,128)(2,1)S(1)}, u32[]{:S(2)}, u32[]{:S(2)}) collective-permute-start(bf16[32,512]{1,0:T(8,128)(2,1)S(1)} %get-tuple-element.68.before), channel_id=1, source_target_pairs={{0,8},{1,9},{2,10},{3,11},{4,12},{5,13},{6,14},{7,15},{8,0},{9,1},... | collective-permute-start | bytes 98312 | tf_op jit(solution)/shard_map/ppermute | solution.py:746
  80.9 4.2 %collective-permute-start.7 = (bf16[48,512]{1,0:T(8,128)(2,1)S(1)}, bf16[48,512]{1,0:T(8,128)(2,1)S(1)}, u32[]{:S(2)}, u32[]{:S(2)}) collective-permute-start(bf16[48,512]{1,0:T(8,128)(2,1)S(1)} %get-tuple-element.70.before), channel_id=1, source_target_pairs={{0,4},{1,5},{2,6},{3,7},{4,0},{5,1},{6,2},{7,3},{8,12},{9,13},{10,... | collective-permute-start | bytes 147464 | tf_op jit(solution)/shard_map/ppermute | solution.py:746
  85.0 4.5 %collective-permute-start.8 = (bf16[80,512]{1,0:T(8,128)(2,1)S(1)}, bf16[80,512]{1,0:T(8,128)(2,1)S(1)}, u32[]{:S(2)}, u32[]{:S(2)}) collective-permute-start(bf16[80,512]{1,0:T(8,128)(2,1)S(1)} %get-tuple-element.72.before), channel_id=1, source_target_pairs={{0,1},{1,0},{2,3},{3,2},{4,5},{5,4},{6,7},{7,6},{8,9},{9,8},{10,11... | collective-permute-start | bytes 245768 | tf_op jit(solution)/shard_map/ppermute | solution.py:746
  89.6 5.2 %collective-permute-start.9 = (bf16[144,512]{1,0:T(8,128)(2,1)S(1)}, bf16[144,512]{1,0:T(8,128)(2,1)S(1)}, u32[]{:S(2)}, u32[]{:S(2)}) collective-permute-start(bf16[144,512]{1,0:T(8,128)(2,1)S(1)} %get-tuple-element.74.before), channel_id=1, source_target_pairs={{0,2},{1,3},{2,0},{3,1},{4,6},{5,7},{6,4},{7,5},{8,10},{9,11},{10,... | collective-permute-start | bytes 442376 | tf_op jit(solution)/shard_map/ppermute | solution.py:746
  98.1 2.7 %copy-start.3 = (bf16[8,256,512]{2,1,0:T(8,128)(2,1)S(1)}, bf16[8,256,512]{2,1,0:T(8,128)(2,1)}, u32[]{:S(2)}) copy-start(bf16[8,256,512]{2,1,0:T(8,128)(2,1)} %get-tuple-element.55) | copy-start | bytes 6291460
  99.4 9.9 %collective-permute-start.17 = (bf16[384,512]{1,0:T(8,128)(2,1)S(1)}, bf16[384,512]{1,0:T(8,128)(2,1)S(1)}, u32[]{:S(2)}, u32[]{:S(2)}) collective-permute-start(bf16[384,512]{1,0:T(8,128)(2,1)S(1)} %shard_map.218), channel_id=1, source_target_pairs={{0,4},{1,5},{2,6},{3,7},{4,0},{5,1},{6,2},{7,3},{8,12},{9,13},{10,... | collective-permute-start | bytes 1179656 | tf_op jit(solution)/shard_map/ppermute | solution.py:704
  102.1 7.4 %copy-start.4 = (bf16[1,8,256,512]{3,2,1,0:T(8,128)(2,1)}, bf16[1,8,256,512]{3,2,1,0:T(8,128)(2,1)S(1)}, u32[]{:S(2)}) copy-start(bf16[1,8,256,512]{3,2,1,0:T(8,128)(2,1)S(1)} %bitcast_dynamic-update-slice_fusion.1) | copy-start | bytes 6291460
  102.1 9.7 %copy-start.5 = (bf16[8,256,512]{2,1,0:T(8,128)(2,1)S(1)}, bf16[8,256,512]{2,1,0:T(8,128)(2,1)}, u32[]{:S(2)}) copy-start(bf16[8,256,512]{2,1,0:T(8,128)(2,1)} %get-tuple-element.64) | copy-start | bytes 6291460
  109.4 8.7 %collective-permute-start.18 = (bf16[192,512]{1,0:T(8,128)(2,1)S(1)}, bf16[192,512]{1,0:T(8,128)(2,1)S(1)}, u32[]{:S(2)}, u32[]{:S(2)}) collective-permute-start(bf16[192,512]{1,0:T(8,128)(2,1)S(1)} %shard_map.219), channel_id=1, source_target_pairs={{0,8},{1,9},{2,10},{3,11},{4,12},{5,13},{6,14},{7,15},{8,0},{9,1},... | collective-permute-start | bytes 589832 | tf_op jit(solution)/shard_map/ppermute | solution.py:704
  113.1 5.9 %copy-start.6 = (bf16[1,8,256,512]{3,2,1,0:T(8,128)(2,1)}, bf16[1,8,256,512]{3,2,1,0:T(8,128)(2,1)S(1)}, u32[]{:S(2)}) copy-start(bf16[1,8,256,512]{3,2,1,0:T(8,128)(2,1)S(1)} %bitcast_dynamic-update-slice_fusion) | copy-start | bytes 6291460
where the time goes:
time: 120 us; the launch traced here: 119 us
  Pallas kernels  53.6 us (45%)
  waiting for transfers between devices  34.3 us (29%)
  starting transfers between devices  17 us (14%)
  other arithmetic  10.4 us (9%)
  local copies, waits for them, and re-layouts  2.69 us (2%)
    pallas_call x1, Pallas kernels, local(): pl.pallas_call(main_body, out_shape=[small_struct, small_struct, half_str...  35.2 us
    ppermute x5, waiting for transfers between devices, exchanged(): return lax.ppermute(packet, PAIR, moves)  15.7 us
    ppermute x4, waiting for transfers between devices, halved(): lax.ppermute(rows_packet, 'dp', [(i, i ^ 1 << GATHER[hop]) for i in range...  13.4 us
    pallas_call x1, Pallas kernels, local(): pl.pallas_call(last_body, grid_spec=pltpu.PrefetchScalarGridSpec(num_scal...  9.95 us
    ppermute x5, starting transfers between devices, exchanged(): return lax.ppermute(packet, PAIR, moves)  8.32 us
    pallas_call x9, Pallas kernels, small_call(): pl.pallas_call(body, out_shape=outs, in_specs=[SMEM] * len(scalars) + (sp...  6.06 us
    ppermute x4, starting transfers between devices, halved(): lax.ppermute(rows_packet, 'dp', [(i, i ^ 1 << GATHER[hop]) for i in range...  5.65 us
    add x4, other arithmetic, halved(): part(totals[b], first, rows) + part(latest[b], bases[b] + first, rows)  4.02 us
  transfers between devices with their start and end apart: 19, of which 9 were waited for; matrix products, arithmetic and copies ran while one was open for 11% of the time, Pallas kernels for 15%

commit v1 on v0

--- a/solution.py
+++ b/solution.py
@@ -22,7 +22,7 @@
 VMEM = pl.BlockSpec(memory_space=pltpu.VMEM)
 SMEM = pl.BlockSpec(memory_space=pltpu.SMEM)
 
-TAPS, CONV, UPB, DOWNB, GAIN, SCALE, SHIFT, SMALL = 0, 7, 8, 11, 12, 16, 20, 24
+TAPS, CONV, UPB, DOWNB, GAIN, CODE, SCALE, SHIFT, SMALL = 0, 7, 8, 11, 12, 13, 16, 20, 24
 
 
 def position(block, order):
@@ -79,7 +79,7 @@
     return adapted, normed.astype(BF16), jnp.broadcast_to(inv, (x.shape[0], 128))
 
 
-def prep_body(sec, speaker, taps, conv, upb, downb, gain, scale_hbm, shift_hbm, own, other, sems):
+def prep_body(sec, place, speaker, taps, conv, upb, downb, gain, scale_hbm, shift_hbm, own, other, sems):
     width = own.shape[1]
     half = SMALL - SHIFT
     copies = []
@@ -106,6 +106,14 @@
         out[DOWNB : DOWNB + 1] = downb[...]
         out[GAIN : GAIN + 1] = gain[...]
         out[GAIN + 1 : SCALE] = jnp.zeros((SCALE - GAIN - 1, width), F32)
+    lane = lax.broadcasted_iota(jnp.int32, (1, width), 1)
+    here = (lane >> 4) == gather_slot((sec[0], place[0]))
+    which = ((lane >> 3) & 1) * 4 + (lane & 3)
+    code = jnp.zeros(lane.shape, jnp.int32)
+    for c in range(2 * half):
+        code = jnp.where(here & (which == c), speaker[c], code)
+    own[CODE : CODE + 1] = (code >> 6).astype(F32)
+    own[CODE + 1 : CODE + 2] = (code & 63).astype(F32)
     for copy in copies:
         copy.wait()
 
@@ -379,7 +387,8 @@
 
 
 def last_body(
-    sec, gpre, up_own, up_got, normed, inv, small, grad_out, tokens, sums0, sums1, gin, away, own, send,
+    sec, gpre, up_own, up_got, normed, inv, small, grad_out, tokens, sums0, sums1, own_small, gin, away, own,
+    send,
     up, shifts, sums, sem,
 ):
     clip = pl.program_id(0)
@@ -415,6 +424,7 @@
     @pl.when(clip == pl.num_programs(0) - 1)
     def _():
         own[...] = pick(sec[0] == 0, sums[...], sums1[...])
+        own[CODE : CODE + 2] = own_small[CODE : CODE + 2]
         send[...] = pick(sec[0] == 0, sums1[...], sums[...])
 
 
@@ -473,27 +483,12 @@
     down[...] = total1[...] + came[share : 2 * share].astype(F32)
 
 
-def begin_rows_body(sec, place, speaker, own_sums, got_sums, packet, smalls, held, sems):
-    spot = (sec[0], place[0])
-    first = spot[0] == 0
-    copies = []
-    for n, source in enumerate((own_sums, got_sums)):
-        fetch(copies, source, 0, SMALL, held.at[n], sems.at[n])
-    for copy in copies:
-        copy.wait()
-    own, other = held[0], held[1]
-    low = pick(first, own[SCALE:], other[SCALE:])
-    high = pick(first, other[SCALE:], own[SCALE:])
+def begin_rows_body(sec, own, got, packet, smalls):
+    first = sec[0] == 0
+    low = pick(first, own[SCALE:], got[SCALE:])
+    high = pick(first, got[SCALE:], own[SCALE:])
     packet[:16] = jnp.concatenate([low, high], axis=0).astype(BF16)
-    lane = lax.broadcasted_iota(jnp.int32, (1, own.shape[1]), 1)
-    here = (lane >> 4) == gather_slot(spot)
-    which = ((lane >> 3) & 1) * 4 + (lane & 3)
-    code = jnp.zeros(lane.shape, jnp.int32)
-    for c in range(8):
-        code = jnp.where(here & (which == c), speaker[c], code)
-    smalls[...] = own[:SCALE] + other[:SCALE]
-    smalls[13:14] = (code >> 6).astype(F32)
-    smalls[14:15] = (code & 63).astype(F32)
+    smalls[...] = own[:SCALE] + got[:SCALE]
     packet[16:32] = smalls[...].astype(BF16)
 
 
@@ -514,7 +509,7 @@
     total = smalls_in[...] + after[size:].astype(F32)
     owned = scale.shape[0]
     count = 2 * size
-    who = total[13:14, :count] * 64.0 + total[14:15, :count]
+    who = total[CODE : CODE + 1, :count] * 64.0 + total[CODE + 1 : CODE + 2, :count]
     wanted = lax.broadcasted_iota(jnp.int32, (owned, count), 0) + place[0] * owned
     hit = who == wanted.astype(F32)
     kind = (lax.broadcasted_iota(jnp.int32, (owned, count), 1) >> 2) & 1
@@ -562,13 +557,13 @@
     own_small, other_small = pl.pallas_call(
         prep_body,
         out_shape=[struct((SMALL, width), F32)] * 2,
-        in_specs=[SMEM, SMEM] + [VMEM] * 5 + [ANY] * 2,
+        in_specs=[SMEM, SMEM, SMEM] + [VMEM] * 5 + [ANY] * 2,
         out_specs=[VMEM] * 2,
         scratch_shapes=[pltpu.SemaphoreType.DMA((2, 2, half))],
         compiler_params=params(),
         name="prep",
     )(
-        sec, speaker, conv_weight.transpose(1, 0, 2), conv_bias, up_bias, down_bias, layer_scale,
+        sec, place[None], speaker, conv_weight.transpose(1, 0, 2), conv_bias, up_bias, down_bias, layer_scale,
         scale_table, shift_table,
     )
     got_small = lax.ppermute(other_small, "section", swap)
@@ -660,6 +655,7 @@
                 pl.BlockSpec(clip_block, lambda c, sec: (sec[0] * half + c, 0, 0)),
                 whole_small,
                 whole_small,
+                whole_small,
             ],
             out_specs=[
                 pl.BlockSpec(clip_block, lambda c, sec: (sec[0] * half + c, 0, 0)),
@@ -678,7 +674,7 @@
         compiler_params=params(),
         cost_estimate=cost(2 * half * product, 12 << 20),
         name="last",
-    )(sec, gpre0, up_own, up_got, normed0, inv0, small0, gin1, tokens, sums0, sums1)
+    )(sec, gpre0, up_own, up_got, normed0, inv0, small0, gin1, tokens, sums0, sums1, own_small)
     got_gin = lax.ppermute(gin_send, "section", swap)
     got_sums = lax.ppermute(sums_send, "section", swap)
 
@@ -688,7 +684,7 @@
     block_outputs = joined(out_own, got_out)
     input_grads = joined(gin_own, got_gin)
     if devices == BLOCKS:
-        outs = halved(sec, place[None], speaker, pairs, own_sums, got_sums, table_rows)
+        outs = halved(sec, place[None], pairs, own_sums, got_sums, table_rows)
     else:
         outs = scattered(section, place, devices, speaker, pairs, own_sums, got_sums, table_rows)
     return (block_outputs, input_grads) + outs
@@ -704,7 +700,7 @@
     return lax.ppermute(packet, PAIR, moves)
 
 
-def halved(sec, place, speaker, pairs, own_sums, got_sums, table_rows):
+def halved(sec, place, pairs, own_sums, got_sums, table_rows):
     _, share, width = pairs[0][0].shape
     pairs = [[piece.reshape(-1, width) for piece in pair] for pair in pairs]
     spot = (sec[0], place[0])
@@ -737,11 +733,7 @@
     def row_outs(hop):
         return [struct(((16 << hop) + 16, width), BF16), struct((SCALE, width), F32)]
 
-    rows_packet, smalls = small_call(
-        begin_rows_body, row_outs(0), [sec, place, speaker],
-        [own_sums, got_sums],
-        [pltpu.VMEM((2, SMALL, width), F32), pltpu.SemaphoreType.DMA((2,))], [HBM] * 2,
-    )
+    rows_packet, smalls = small_call(begin_rows_body, row_outs(0), [sec], [own_sums, got_sums], limit=None)
     for hop in range(len(GATHER)):
         more = lax.ppermute(
             rows_packet, "dp", [(i, i ^ (1 << GATHER[hop])) for i in range(BLOCKS)]

time: 120 us -> 123 us (1.025)
  local copies, waits for them, and re-layouts: 2.69 us -> 4.22 us
    unnamed x16 -> x22, local copies, waits for them, and re-layouts: 0.04 us -> 1.56 us
where the time goes in v1:
time: 123 us; the launch traced here: 122 us
  Pallas kernels  54.5 us (44%)
  waiting for transfers between devices  34.4 us (28%)
  starting transfers between devices  17 us (14%)
  other arithmetic  10.6 us (9%)
  local copies, waits for them, and re-layouts  4.22 us (3%)
    pallas_call x1, Pallas kernels, local(): pl.pallas_call(main_body, out_shape=[small_struct, small_struct, half_str...  35.2 us
    ppermute x5, waiting for transfers between devices, exchanged(): return lax.ppermute(packet, PAIR, moves)  15.6 us
    ppermute x4, waiting for transfers between devices, halved(): lax.ppermute(rows_packet, 'dp', [(i, i ^ 1 << GATHER[hop]) for i in range...  13.6 us
    pallas_call x1, Pallas kernels, local(): pl.pallas_call(last_body, grid_spec=pltpu.PrefetchScalarGridSpec(num_scal...  10 us
    ppermute x5, starting transfers between devices, exchanged(): return lax.ppermute(packet, PAIR, moves)  8.35 us
    pallas_call x9, Pallas kernels, small_call(): pl.pallas_call(body, out_shape=outs, in_specs=[SMEM] * len(scalars) + (sp...  6.9 us
    ppermute x4, starting transfers between devices, halved(): lax.ppermute(rows_packet, 'dp', [(i, i ^ 1 << GATHER[hop]) for i in range...  5.64 us
    add x4, other arithmetic, halved(): part(totals[b], first, rows) + part(latest[b], bases[b] + first, rows)  4.26 us
  transfers between devices with their start and end apart: 19, of which 9 were waited for; matrix products, arithmetic and copies ran while one was open for 11% of the time, Pallas kernels for 15%

profile of v1, /device:TPU:0, one launch (start us, length us, event | category | flops | bytes accessed | tf_op | source)
XLA Modules:
  0.0 121.8 jit_solution(4353388589765938608)
XLA Ops:
  0.6 0.6 collective-permute-start.1
  1.2 0.1 collective-permute-start.2
  1.3 2.4 %prep.1 = (f32[24,512]{1,0:T(8,128)}, f32[24,512]{1,0:T(8,128)}) custom-call(s32[1]{0:T(128)} %bitcast.sec, s32[1]{0:T(128)} %bitcast.1.place, s32[8]{0:T(128)} %speaker.1, f32[7,1,512]{2,1,0:T(1,128)} %bitcast.30, f32[1,512]{1,0:T(1,128)} %conv.1, f32[1,1536]{1,0:T(1,128)} %upb.1, f32[1,512]{1,0:T(1,128)} %downb.1, f32[1,512]{1,0:T(1,128)} %gain.1, ...), custom_call_target="tpu_custom_call" | custom-call | tf_op jit(solution)/shard_map/prep/pallas_call | solution.py:557
  3.7 0.5 collective-permute-start
  4.2 2.7 %collective-permute-done.got_small = f32[24,512]{1,0:T(8,128)} collective-permute-done((f32[24,512]{1,0:T(8,128)}, f32[24,512]{1,0:T(8,128)}, u32[]{:S(2)}, u32[]{:S(2)}) %collective-permute-start) | collective-permute-done | bytes 49184 | tf_op jit(solution)/shard_map/ppermute | solution.py:569
  6.9 35.2 %main.1 = (f32[24,512]{1,0:T(8,128)}, f32[24,512]{1,0:T(8,128)}, bf16[4,256,512]{2,1,0:T(8,128)(2,1)}, bf16[1024,512]{1,0:T(8,128)(2,1)}, f32[1024,128]{1,0:T(8,...) custom-call(s32[1]{0:T(128)} %bitcast.sec, ...), custom_call_target="tpu_custom_call" | custom-call | flops 17716740096 | bytes 25165824 | tf_op jit(solution)/shard_map/main/pallas_call | solution.py:590
  42.1 0.4 collective-permute-start.14
  42.5 0.2 collective-permute-start.11
  42.7 0.3 collective-permute-start.3
  43.0 0.2 collective-permute-start.13
  43.2 0.3 collective-permute-start.10
  43.5 1.3 %dynamic-slice_convert_fusion = f32[768,512]{1,0:T(8,128)S(1)} fusion(bf16[1536,512]{1,0:T(8,128)(2,1)} %bitcast.28, s32[]{:T(128)S(6)} %select_n.53), kind=kLoop, calls=%fused_computation.9 | loop fusion | flops 393216 | bytes 2359300 | tf_op jit(solution)/shard_map/convert_element_type | solution.py:710
  44.9 0.2 dynamic-slice_convert_fusion.1
  45.1 1.2 %fusion = bf16[768,512]{1,0:T(8,128)(2,1)} fusion(f32[768,512]{1,0:T(8,128)S(1)} %dynamic-slice_convert_fusion, bf16[8,96,512]{2,1,0:T(8,128)(2,1)S(1)} %collective-permute-done.14), kind=kLoop, calls=%fused_computation.1 | loop fusion | flops 1179648 | bytes 3145728 | tf_op jit(solution)/shard_map/convert_element_type | solution.py:717
  46.4 2.6 %collective-permute-start.15 = (bf16[768,512]{1,0:T(8,128)(2,1)}, bf16[768,512]{1,0:T(8,128)(2,1)}, u32[]{:S(2)}, u32[]{:S(2)}) collective-permute-start(bf16[768,512]{1,0:T(8,128)(2,1)} %fusion), channel_id=1, source_target_pairs={{0,1},{1,0},{2,3},{3,2},{4,5},{5,4},{6,7},{7,6},{8,9},{9,8},{10,11... | collective-permute-start | bytes 2359304 | tf_op jit(solution)/shard_map/ppermute | solution.py:700
  49.0 1.3 %fusion.1 = bf16[768,512]{1,0:T(8,128)(2,1)} fusion(f32[768,512]{1,0:T(8,128)S(1)} %dynamic-slice_convert_fusion.1, bf16[8,96,512]{2,1,0:T(8,128)(2,1)S(1)} %collective-permute-done.11), kind=kLoop, calls=%fused_computation.3 | loop fusion | flops 1179648 | bytes 3145728 | tf_op jit(solution)/shard_map/convert_element_type | solution.py:717
  50.3 10.0 %last.1 = (bf16[8,256,512]{2,1,0:T(8,128)(2,1)}, bf16[4,256,512]{2,1,0:T(8,128)(2,1)}, f32[24,512]{1,0:T(8,128)}, f32[24,512]{1,0:T(8,128)}) custom-call(s32[1]{0:T(128)} %bitcast.sec, bf16[3,1024,512]{2,1,0:T(8,128)(2,1)} %get-tuple-element.57.gpre, bf16[512,1536]{1,0:T(8,128)(2,1)} %bitcast.37, bf16[512,1536]{1,0:T(8,128)(2,1)} %collective-permute-done.1.up_got, ...), custom_call_target="tpu_custom_call" | custom-call | flops 12884901888 | bytes 12582912 | tf_op jit(solution)/shard_map/last/pallas_call | solution.py:642
  60.3 2.3 %convert_add_fusion.2 = (f32[768,512]{1,0:T(8,128)S(1)}, f32[768,512]{1,0:T(8,128)S(1)}) fusion(bf16[768,512]{1,0:T(8,128)(2,1)} %bitcast.16, bf16[1536,512]{1,0:T(8,128)(2,1)} %bitcast.29, s32[]{:T(128)S(6)} %select_n.50, bf16[768,512]{1,0:T(8,128)(2,1)} %bitcast.13, bf16[1536,512]{1,0:T(8,128)(2,1)} %bitcast.26), kind=kLoop, calls=%fused_computation.4 | loop fusion | flops 2359296 | bytes 6291460 | tf_op jit(solution)/shard_map/add | solution.py:720
  62.6 0.0 copy-start.2
  62.7 5.0 %collective-permute-done.12.refs_0_ = bf16[768,512]{1,0:T(8,128)(2,1)} collective-permute-done((bf16[768,512]{1,0:T(8,128)(2,1)}, bf16[768,512]{1,0:T(8,128)(2,1)}, u32[]{:S(2)}, u32[]{:S(2)}) %collective-permute-start.12) | collective-permute-done | bytes 786464 | tf_op jit(solution)/shard_map/ppermute | solution.py:700
  67.7 2.2 %shard_map.217 = bf16[768,512]{1,0:T(8,128)(2,1)} custom-call(s32[1]{0:T(128)} %bitcast.sec, s32[1]{0:T(128)} %bitcast.1.place, f32[768,512]{1,0:T(8,128)S(1)} %get-tuple-element.100.total0, f32[768,512]{1,0:T(8,128)S(1)} %get-tuple-element.99.total1, bf16[768,512]{1,0:T(8,128)(2,1)} %collective-permute-done.12.refs_0_, ...), custom_call_target="tpu_custom_call" | custom-call | bytes 2097152 | tf_op jit(solution)/shard_map/pallas_call | solution.py:723
  69.9 2.1 %collective-permute-start.16 = (bf16[768,512]{1,0:T(8,128)(2,1)}, bf16[768,512]{1,0:T(8,128)(2,1)}, u32[]{:S(2)}, u32[]{:S(2)}) collective-permute-start(bf16[768,512]{1,0:T(8,128)(2,1)} %shard_map.217), channel_id=1, source_target_pairs={{0,2},{1,3},{2,0},{3,1},{4,6},{5,7},{6,4},{7,5},{8,10},{9,11},{10,... | collective-permute-start | bytes 2359304 | tf_op jit(solution)/shard_map/ppermute | solution.py:700
  72.0 0.5 collective-permute-start.5
  72.5 2.6 %collective-permute-done.5.got = f32[24,512]{1,0:T(8,128)} collective-permute-done((f32[24,512]{1,0:T(8,128)S(1)}, f32[24,512]{1,0:T(8,128)}, u32[]{:S(2)}, u32[]{:S(2)}) %collective-permute-start.5) | collective-permute-done | bytes 49184 | tf_op jit(solution)/shard_map/ppermute | solution.py:679
  75.1 1.5 %shard_map.212 = (bf16[32,512]{1,0:T(8,128)(2,1)}, f32[16,512]{1,0:T(8,128)}) custom-call(s32[1]{0:T(128)} %bitcast.sec, f32[24,512]{1,0:T(8,128)} %get-tuple-element.66.own, f32[24,512]{1,0:T(8,128)} %collective-permute-done.5.got), custom_call_target="tpu_custom_call" | custom-call | bytes 2097152 | tf_op jit(solution)/shard_map/pallas_call | solution.py:723
  76.5 2.6 %collective-permute-start.6 = (bf16[32,512]{1,0:T(8,128)(2,1)}, bf16[32,512]{1,0:T(8,128)(2,1)S(1)}, u32[]{:S(2)}, u32[]{:S(2)}) collective-permute-start(bf16[32,512]{1,0:T(8,128)(2,1)} %get-tuple-element.68.before), channel_id=1, source_target_pairs={{0,8},{1,9},{2,10},{3,11},{4,12},{5,13},{6,14},{7,15},{8,0},{9,1},... | collective-permute-start | bytes 98312 | tf_op jit(solution)/shard_map/ppermute | solution.py:738
  79.1 2.8 %collective-permute-done.6.after = bf16[32,512]{1,0:T(8,128)(2,1)S(1)} collective-permute-done((bf16[32,512]{1,0:T(8,128)(2,1)}, bf16[32,512]{1,0:T(8,128)(2,1)S(1)}, u32[]{:S(2)}, u32[]{:S(2)}) %collective-permute-start.6) | collective-permute-done | bytes 32800 | tf_op jit(solution)/shard_map/ppermute | solution.py:738
  81.9 0.8 copy-done.3
  82.7 0.8 copy-done.4
  83.4 1.3 %collective-permute-start.7 = (bf16[48,512]{1,0:T(8,128)(2,1)S(1)}, bf16[48,512]{1,0:T(8,128)(2,1)S(1)}, u32[]{:S(2)}, u32[]{:S(2)}) collective-permute-start(bf16[48,512]{1,0:T(8,128)(2,1)S(1)} %get-tuple-element.70.before), channel_id=1, source_target_pairs={{0,4},{1,5},{2,6},{3,7},{4,0},{5,1},{6,2},{7,3},{8,12},{9,13},{10,... | collective-permute-start | bytes 147464 | tf_op jit(solution)/shard_map/ppermute | solution.py:738
  84.7 2.9 %collective-permute-done.7.after = bf16[48,512]{1,0:T(8,128)(2,1)S(1)} collective-permute-done((bf16[48,512]{1,0:T(8,128)(2,1)S(1)}, bf16[48,512]{1,0:T(8,128)(2,1)S(1)}, u32[]{:S(2)}, u32[]{:S(2)}) %collective-permute-start.7) | collective-permute-done | bytes 49184 | tf_op jit(solution)/shard_map/ppermute | solution.py:738
  87.6 1.6 %collective-permute-start.8 = (bf16[80,512]{1,0:T(8,128)(2,1)S(1)}, bf16[80,512]{1,0:T(8,128)(2,1)S(1)}, u32[]{:S(2)}, u32[]{:S(2)}) collective-permute-start(bf16[80,512]{1,0:T(8,128)(2,1)S(1)} %get-tuple-element.72.before), channel_id=1, source_target_pairs={{0,1},{1,0},{2,3},{3,2},{4,5},{5,4},{6,7},{7,6},{8,9},{9,8},{10,11... | collective-permute-start | bytes 245768 | tf_op jit(solution)/shard_map/ppermute | solution.py:738
  89.2 2.9 %collective-permute-done.8.after = bf16[80,512]{1,0:T(8,128)(2,1)S(1)} collective-permute-done((bf16[80,512]{1,0:T(8,128)(2,1)S(1)}, bf16[80,512]{1,0:T(8,128)(2,1)S(1)}, u32[]{:S(2)}, u32[]{:S(2)}) %collective-permute-start.8) | collective-permute-done | bytes 81952 | tf_op jit(solution)/shard_map/ppermute | solution.py:738
  92.1 0.2 collective-permute-start.9
  92.3 5.0 %collective-permute-done.9.after = bf16[144,512]{1,0:T(8,128)(2,1)S(1)} collective-permute-done((bf16[144,512]{1,0:T(8,128)(2,1)S(1)}, bf16[144,512]{1,0:T(8,128)(2,1)S(1)}, u32[]{:S(2)}, u32[]{:S(2)}) %collective-permute-start.9) | collective-permute-done | bytes 147488 | tf_op jit(solution)/shard_map/ppermute | solution.py:738
  97.3 1.1 shard_map.216
  98.4 1.3 %convert_add_fusion.4.total1 = f32[384,512]{1,0:T(8,128)S(1)} fusion(f32[768,512]{1,0:T(8,128)} %copy-done.2, s32[]{:T(128)S(6)} %select_n.52, bf16[768,512]{1,0:T(8,128)(2,1)} %collective-permute-done.15.refs_1_), kind=kLoop, calls=%fused_computation.8 | loop fusion | flops 393216 | bytes 1966084 | tf_op jit(solution)/shard_map/add | solution.py:785
  99.8 1.1 convert_add_fusion.5.total0
  100.9 1.3 %shard_map.218 = bf16[384,512]{1,0:T(8,128)(2,1)S(1)} custom-call(s32[1]{0:T(128)} %bitcast.sec, s32[1]{0:T(128)} %bitcast.1.place, f32[384,512]{1,0:T(8,128)S(1)} %convert_add_fusion.5.total0, f32[384,512]{1,0:T(8,128)S(1)} %convert_add_fusion.4.total1, bf16[768,512]{1,0:T(8,128)(2,1)} %collective-permute-done.16.refs_0_), custom_call_target="tpu_custom_call" | custom-call | bytes 2097152 | tf_op jit(solution)/shard_map/pallas_call | solution.py:723
  102.2 1.3 %collective-permute-start.17 = (bf16[384,512]{1,0:T(8,128)(2,1)S(1)}, bf16[384,512]{1,0:T(8,128)(2,1)S(1)}, u32[]{:S(2)}, u32[]{:S(2)}) collective-permute-start(bf16[384,512]{1,0:T(8,128)(2,1)S(1)} %shard_map.218), channel_id=1, source_target_pairs={{0,4},{1,5},{2,6},{3,7},{4,0},{5,1},{6,2},{7,3},{8,12},{9,13},{10,... | collective-permute-start | bytes 1179656 | tf_op jit(solution)/shard_map/ppermute | solution.py:700
  103.6 1.3 %bitcast_dynamic-update-slice_fusion.1 = bf16[1,8,256,512]{3,2,1,0:T(8,128)(2,1)S(1)} fusion(bf16[1,8,256,512]{3,2,1,0:T(8,128)(2,1)S(1)} %bitcast.31, s32[]{:T(128)S(6)} %select_n.48, bf16[4,256,512]{2,1,0:T(8,128)(2,1)} %collective-permute-done.3), kind=kLoop, calls=%fused_computation.7 | loop fusion | bytes 2097156 | tf_op jit(solution)/shard_map/dynamic_update_slice | solution.py:682
  104.9 1.7 %convert_add_fusion.6 = (f32[192,512]{1,0:T(8,128)S(1)}, f32[192,512]{1,0:T(8,128)S(1)}) fusion(f32[384,512]{1,0:T(8,128)S(1)} %convert_add_fusion.4.total1, s32[]{:T(128)S(6)} %select_n.55, bf16[768,512]{1,0:T(8,128)(2,1)} %collective-permute-done.16.refs_0_, s32[]{:T(128)S(6)} %select_n.59, s32[]{:T(128)S(6)} %select_n.56, ...), kind=kLoop, calls=%fused_computation.12 | loop fusion | flops 393216 | bytes 1966092 | tf_op jit(solution)/shard_map/add | solution.py:785
  106.7 5.5 %collective-permute-done.17.refs_0_ = bf16[384,512]{1,0:T(8,128)(2,1)S(1)} collective-permute-done((bf16[384,512]{1,0:T(8,128)(2,1)S(1)}, bf16[384,512]{1,0:T(8,128)(2,1)S(1)}, u32[]{:S(2)}, u32[]{:S(2)}) %collective-permute-start.17) | collective-permute-done | bytes 393248 | tf_op jit(solution)/shard_map/ppermute | solution.py:700
  112.2 2.3 %collective-permute-start.18 = (bf16[192,512]{1,0:T(8,128)(2,1)S(1)}, bf16[192,512]{1,0:T(8,128)(2,1)S(1)}, u32[]{:S(2)}, u32[]{:S(2)}) collective-permute-start(bf16[192,512]{1,0:T(8,128)(2,1)S(1)} %shard_map.219), channel_id=1, source_target_pairs={{0,8},{1,9},{2,10},{3,11},{4,12},{5,13},{6,14},{7,15},{8,0},{9,1},... | collective-permute-start | bytes 589832 | tf_op jit(solution)/shard_map/ppermute | solution.py:700
  114.6 1.3 %bitcast_dynamic-update-slice_fusion = bf16[1,8,256,512]{3,2,1,0:T(8,128)(2,1)S(1)} fusion(bf16[1,8,256,512]{3,2,1,0:T(8,128)(2,1)S(1)} %bitcast.32, s32[]{:T(128)S(6)} %select_n.48, bf16[4,256,512]{2,1,0:T(8,128)(2,1)} %collective-permute-done.4), kind=kLoop, calls=%fused_computation.6 | loop fusion | bytes 2097156 | tf_op jit(solution)/shard_map/dynamic_update_slice | solution.py:682
  115.9 0.1 convert_add_fusion.8
  116.0 5.0 %collective-permute-done.18.came = bf16[192,512]{1,0:T(8,128)(2,1)S(1)} collective-permute-done((bf16[192,512]{1,0:T(8,128)(2,1)S(1)}, bf16[192,512]{1,0:T(8,128)(2,1)S(1)}, u32[]{:S(2)}, u32[]{:S(2)}) %collective-permute-start.18) | collective-permute-done | bytes 196640 | tf_op jit(solution)/shard_map/ppermute | solution.py:700
  121.0 0.8 shard_map.220
  (35 shorter events, 0.1 us)
Async XLA Ops:
  0.6 6.3 %collective-permute-start.1 = (bf16[512,1536]{1,0:T(8,128)(2,1)}, bf16[512,1536]{1,0:T(8,128)(2,1)}, u32[]{:S(2)}, u32[]{:S(2)}) collective-permute-start(bf16[512,1536]{1,0:T(8,128)(2,1)} %bitcast.35), channel_id=1, source_target_pairs={{0,16},{16,0},{1,17},{17,1},{2,18},{18,2},{3,19},{19,3},{4,20},{20... | collective-permute-start | bytes 4718600 | tf_op jit(solution)/shard_map/ppermute | solution.py:571
  1.2 5.7 %collective-permute-start.2 = (bf16[1536,512]{1,0:T(8,128)(2,1)}, bf16[1536,512]{1,0:T(8,128)(2,1)}, u32[]{:S(2)}, u32[]{:S(2)}) collective-permute-start(bf16[1536,512]{1,0:T(8,128)(2,1)} %bitcast.33), channel_id=1, source_target_pairs={{0,16},{16,0},{1,17},{17,1},{2,18},{18,2},{3,19},{19,3},{4,20},{20... | collective-permute-start | bytes 4718600 | tf_op jit(solution)/shard_map/ppermute | solution.py:572
  3.7 3.2 %collective-permute-start = (f32[24,512]{1,0:T(8,128)}, f32[24,512]{1,0:T(8,128)}, u32[]{:S(2)}, u32[]{:S(2)}) collective-permute-start(f32[24,512]{1,0:T(8,128)} %get-tuple-element.54), channel_id=1, source_target_pairs={{0,16},{16,0},{1,17},{17,1},{2,18},{18,2},{3,19},{19,3},{4,20},{20... | collective-permute-start | bytes 147464 | tf_op jit(solution)/shard_map/ppermute | solution.py:569
  42.1 2.8 %copy-start.5 = (bf16[16,96,512]{2,1,0:T(8,128)(2,1)S(1)}, bf16[16,96,512]{2,1,0:T(8,128)(2,1)}, u32[]{:S(2)}) copy-start(bf16[16,96,512]{2,1,0:T(8,128)(2,1)} %get-tuple-element.80) | copy-start | bytes 4718596
  42.1 3.0 %collective-permute-start.14 = (bf16[8,96,512]{2,1,0:T(8,128)(2,1)}, bf16[8,96,512]{2,1,0:T(8,128)(2,1)S(1)}, u32[]{:S(2)}, u32[]{:S(2)}) collective-permute-start(bf16[8,96,512]{2,1,0:T(8,128)(2,1)} %get-tuple-element.89), channel_id=1, source_target_pairs={{0,16},{16,0},{1,17},{17,1},{2,18},{18,2},{3,19},{19,3},{4,20},{20... | collective-permute-start | bytes 2359304 | tf_op jit(solution)/shard_map/ppermute | solution.py:638
  42.5 6.5 %collective-permute-start.11 = (bf16[8,96,512]{2,1,0:T(8,128)(2,1)}, bf16[8,96,512]{2,1,0:T(8,128)(2,1)S(1)}, u32[]{:S(2)}, u32[]{:S(2)}) collective-permute-start(bf16[8,96,512]{2,1,0:T(8,128)(2,1)} %get-tuple-element.84), channel_id=1, source_target_pairs={{0,16},{16,0},{1,17},{17,1},{2,18},{18,2},{3,19},{19,3},{4,20},{20... | collective-permute-start | bytes 2359304 | tf_op jit(solution)/shard_map/ppermute | solution.py:638
  42.7 60.9 %collective-permute-start.3 = (bf16[4,256,512]{2,1,0:T(8,128)(2,1)}, bf16[4,256,512]{2,1,0:T(8,128)(2,1)}, u32[]{:S(2)}, u32[]{:S(2)}) collective-permute-start(bf16[4,256,512]{2,1,0:T(8,128)(2,1)} %get-tuple-element.56), channel_id=1, source_target_pairs={{0,16},{16,0},{1,17},{17,1},{2,18},{18,2},{3,19},{19,3},{4,20},{20... | collective-permute-start | bytes 3145736 | tf_op jit(solution)/shard_map/ppermute | solution.py:640
  43.0 17.2 %collective-permute-start.13 = (bf16[8,96,512]{2,1,0:T(8,128)(2,1)}, bf16[8,96,512]{2,1,0:T(8,128)(2,1)}, u32[]{:S(2)}, u32[]{:S(2)}) collective-permute-start(bf16[8,96,512]{2,1,0:T(8,128)(2,1)} %get-tuple-element.86), channel_id=1, source_target_pairs={{0,16},{16,0},{1,17},{17,1},{2,18},{18,2},{3,19},{19,3},{4,20},{20... | collective-permute-start | bytes 2359304 | tf_op jit(solution)/shard_map/ppermute | solution.py:638
  43.2 17.1 %collective-permute-start.10 = (bf16[8,96,512]{2,1,0:T(8,128)(2,1)}, bf16[8,96,512]{2,1,0:T(8,128)(2,1)}, u32[]{:S(2)}, u32[]{:S(2)}) collective-permute-start(bf16[8,96,512]{2,1,0:T(8,128)(2,1)} %get-tuple-element.81), channel_id=1, source_target_pairs={{0,16},{16,0},{1,17},{17,1},{2,18},{18,2},{3,19},{19,3},{4,20},{20... | collective-permute-start | bytes 2359304 | tf_op jit(solution)/shard_map/ppermute | solution.py:638
  46.4 16.3 %collective-permute-start.15 = (bf16[768,512]{1,0:T(8,128)(2,1)}, bf16[768,512]{1,0:T(8,128)(2,1)}, u32[]{:S(2)}, u32[]{:S(2)}) collective-permute-start(bf16[768,512]{1,0:T(8,128)(2,1)} %fusion), channel_id=1, source_target_pairs={{0,1},{1,0},{2,3},{3,2},{4,5},{5,4},{6,7},{7,6},{8,9},{9,8},{10,11... | collective-permute-start | bytes 2359304 | tf_op jit(solution)/shard_map/ppermute | solution.py:700
  50.3 17.4 %collective-permute-start.12 = (bf16[768,512]{1,0:T(8,128)(2,1)}, bf16[768,512]{1,0:T(8,128)(2,1)}, u32[]{:S(2)}, u32[]{:S(2)}) collective-permute-start(bf16[768,512]{1,0:T(8,128)(2,1)} %fusion.1), channel_id=1, source_target_pairs={{0,1},{1,0},{2,3},{3,2},{4,5},{5,4},{6,7},{7,6},{8,9},{9,8},{10,11... | collective-permute-start | bytes 2359304 | tf_op jit(solution)/shard_map/ppermute | solution.py:700
  62.6 7.3 %copy-start = (f32[768,512]{1,0:T(8,128)}, f32[768,512]{1,0:T(8,128)S(1)}, u32[]{:S(2)}) copy-start(f32[768,512]{1,0:T(8,128)S(1)} %get-tuple-element.100.total0) | copy-start | bytes 4718596
  62.6 7.3 %copy-start.2 = (f32[768,512]{1,0:T(8,128)}, f32[768,512]{1,0:T(8,128)S(1)}, u32[]{:S(2)}) copy-start(f32[768,512]{1,0:T(8,128)S(1)} %get-tuple-element.99.total1) | copy-start | bytes 4718596
  67.7 4.3 %copy-start.10 = (f32[24,512]{1,0:T(8,128)S(1)}, f32[24,512]{1,0:T(8,128)}, u32[]{:S(2)}) copy-start(f32[24,512]{1,0:T(8,128)} %get-tuple-element.67) | copy-start | bytes 147460
  69.9 31.0 %collective-permute-start.16 = (bf16[768,512]{1,0:T(8,128)(2,1)}, bf16[768,512]{1,0:T(8,128)(2,1)}, u32[]{:S(2)}, u32[]{:S(2)}) collective-permute-start(bf16[768,512]{1,0:T(8,128)(2,1)} %shard_map.217), channel_id=1, source_target_pairs={{0,2},{1,3},{2,0},{3,1},{4,6},{5,7},{6,4},{7,5},{8,10},{9,11},{10,... | collective-permute-start | bytes 2359304 | tf_op jit(solution)/shard_map/ppermute | solution.py:700
  72.0 42.6 %collective-permute-start.4 = (bf16[4,256,512]{2,1,0:T(8,128)(2,1)}, bf16[4,256,512]{2,1,0:T(8,128)(2,1)}, u32[]{:S(2)}, u32[]{:S(2)}) collective-permute-start(bf16[4,256,512]{2,1,0:T(8,128)(2,1)} %get-tuple-element.65), channel_id=1, source_target_pairs={{0,16},{16,0},{1,17},{17,1},{2,18},{18,2},{3,19},{19,3},{4,20},{20... | collective-permute-start | bytes 3145736 | tf_op jit(solution)/shard_map/ppermute | solution.py:678
  72.0 3.1 %collective-permute-start.5 = (f32[24,512]{1,0:T(8,128)S(1)}, f32[24,512]{1,0:T(8,128)}, u32[]{:S(2)}, u32[]{:S(2)}) collective-permute-start(f32[24,512]{1,0:T(8,128)S(1)} %copy-done.10), channel_id=1, source_target_pairs={{0,16},{16,0},{1,17},{17,1},{2,18},{18,2},{3,19},{19,3},{4,20},{20... | collective-permute-start | bytes 147464 | tf_op jit(solution)/shard_map/ppermute | solution.py:679
  76.5 23.2 %copy-start.1 = (f32[768,512]{1,0:T(8,128)S(1)}, f32[768,512]{1,0:T(8,128)}, u32[]{:S(2)}) copy-start(f32[768,512]{1,0:T(8,128)} %copy-done) | copy-start | bytes 4718596
  76.5 5.4 %collective-permute-start.6 = (bf16[32,512]{1,0:T(8,128)(2,1)}, bf16[32,512]{1,0:T(8,128)(2,1)S(1)}, u32[]{:S(2)}, u32[]{:S(2)}) collective-permute-start(bf16[32,512]{1,0:T(8,128)(2,1)} %get-tuple-element.68.before), channel_id=1, source_target_pairs={{0,8},{1,9},{2,10},{3,11},{4,12},{5,13},{6,14},{7,15},{8,0},{9,1},... | collective-permute-start | bytes 98312 | tf_op jit(solution)/shard_map/ppermute | solution.py:738
  81.9 0.8 copy-start.3
  82.7 0.8 copy-start.4
  83.4 4.2 %collective-permute-start.7 = (bf16[48,512]{1,0:T(8,128)(2,1)S(1)}, bf16[48,512]{1,0:T(8,128)(2,1)S(1)}, u32[]{:S(2)}, u32[]{:S(2)}) collective-permute-start(bf16[48,512]{1,0:T(8,128)(2,1)S(1)} %get-tuple-element.70.before), channel_id=1, source_target_pairs={{0,4},{1,5},{2,6},{3,7},{4,0},{5,1},{6,2},{7,3},{8,12},{9,13},{10,... | collective-permute-start | bytes 147464 | tf_op jit(solution)/shard_map/ppermute | solution.py:738
  87.6 4.5 %collective-permute-start.8 = (bf16[80,512]{1,0:T(8,128)(2,1)S(1)}, bf16[80,512]{1,0:T(8,128)(2,1)S(1)}, u32[]{:S(2)}, u32[]{:S(2)}) collective-permute-start(bf16[80,512]{1,0:T(8,128)(2,1)S(1)} %get-tuple-element.72.before), channel_id=1, source_target_pairs={{0,1},{1,0},{2,3},{3,2},{4,5},{5,4},{6,7},{7,6},{8,9},{9,8},{10,11... | collective-permute-start | bytes 245768 | tf_op jit(solution)/shard_map/ppermute | solution.py:738
  92.1 5.2 %collective-permute-start.9 = (bf16[144,512]{1,0:T(8,128)(2,1)S(1)}, bf16[144,512]{1,0:T(8,128)(2,1)S(1)}, u32[]{:S(2)}, u32[]{:S(2)}) collective-permute-start(bf16[144,512]{1,0:T(8,128)(2,1)S(1)} %get-tuple-element.74.before), channel_id=1, source_target_pairs={{0,2},{1,3},{2,0},{3,1},{4,6},{5,7},{6,4},{7,5},{8,10},{9,11},{10,... | collective-permute-start | bytes 442376 | tf_op jit(solution)/shard_map/ppermute | solution.py:738
  100.9 2.7 %copy-start.6 = (bf16[8,256,512]{2,1,0:T(8,128)(2,1)S(1)}, bf16[8,256,512]{2,1,0:T(8,128)(2,1)}, u32[]{:S(2)}) copy-start(bf16[8,256,512]{2,1,0:T(8,128)(2,1)} %get-tuple-element.55) | copy-start | bytes 6291460
  102.2 9.9 %collective-permute-start.17 = (bf16[384,512]{1,0:T(8,128)(2,1)S(1)}, bf16[384,512]{1,0:T(8,128)(2,1)S(1)}, u32[]{:S(2)}, u32[]{:S(2)}) collective-permute-start(bf16[384,512]{1,0:T(8,128)(2,1)S(1)} %shard_map.218), channel_id=1, source_target_pairs={{0,4},{1,5},{2,6},{3,7},{4,0},{5,1},{6,2},{7,3},{8,12},{9,13},{10,... | collective-permute-start | bytes 1179656 | tf_op jit(solution)/shard_map/ppermute | solution.py:700
  104.9 7.3 %copy-start.7 = (bf16[1,8,256,512]{3,2,1,0:T(8,128)(2,1)}, bf16[1,8,256,512]{3,2,1,0:T(8,128)(2,1)S(1)}, u32[]{:S(2)}) copy-start(bf16[1,8,256,512]{3,2,1,0:T(8,128)(2,1)S(1)} %bitcast_dynamic-update-slice_fusion.1) | copy-start | bytes 6291460
  104.9 9.7 %copy-start.8 = (bf16[8,256,512]{2,1,0:T(8,128)(2,1)S(1)}, bf16[8,256,512]{2,1,0:T(8,128)(2,1)}, u32[]{:S(2)}) copy-start(bf16[8,256,512]{2,1,0:T(8,128)(2,1)} %get-tuple-element.64) | copy-start | bytes 6291460
  112.2 8.7 %collective-permute-start.18 = (bf16[192,512]{1,0:T(8,128)(2,1)S(1)}, bf16[192,512]{1,0:T(8,128)(2,1)S(1)}, u32[]{:S(2)}, u32[]{:S(2)}) collective-permute-start(bf16[192,512]{1,0:T(8,128)(2,1)S(1)} %shard_map.219), channel_id=1, source_target_pairs={{0,8},{1,9},{2,10},{3,11},{4,12},{5,13},{6,14},{7,15},{8,0},{9,1},... | collective-permute-start | bytes 589832 | tf_op jit(solution)/shard_map/ppermute | solution.py:700
  115.9 5.9 %copy-start.9 = (bf16[1,8,256,512]{3,2,1,0:T(8,128)(2,1)}, bf16[1,8,256,512]{3,2,1,0:T(8,128)(2,1)S(1)}, u32[]{:S(2)}) copy-start(bf16[1,8,256,512]{3,2,1,0:T(8,128)(2,1)S(1)} %bitcast_dynamic-update-slice_fusion) | copy-start | bytes 6291460

commit v2 on v1

--- a/solution.py
+++ b/solution.py
@@ -118,10 +118,12 @@
         copy.wait()
 
 
-def forward_tiles(adapted, up, down, small, act, slope, acc):
+def forward_tiles(adapted, up, down, small, act, slope, acc, before=None, after=None):
     steps = [(j, r) for j in range(3) for r in range(acc.shape[0] // 256)]
 
     def hidden(j, r):
+        if j == 0 and before is not None:
+            before(r)
         part = dot(adapted[r * 256 : (r + 1) * 256], up[:, j * TILE : (j + 1) * TILE], NN)
         return part + small[UPB + j : UPB + j + 1]
 
@@ -137,6 +139,8 @@
         slope[j, rows] = (phi + pre * (DENSITY * jnp.exp(-0.5 * pre * pre))).astype(BF16)
         part = dot(low, down[j * TILE : (j + 1) * TILE], NN)
         acc[rows] = part if j == 0 else acc[rows] + part
+        if j == 2 and after is not None:
+            after(r)
 
 
 def activation_tile(j, gb, down, slope, sums):
@@ -266,7 +270,8 @@
     sec, place, valid, own_small, got_small, tokens, cot, up_own, up_got, down_own, down_got,
     sums0, sums1, gin1, normed_hbm, inv_hbm, out_own, out_send, gpre_hbm, up_keep, down_keep,
     up_pass, down_pass, up_stay, down_stay, small0_out,
-    up0, down0, up1, down1, act0, slope0, act1, slope1, acc, adapted0, normed, inv, adapted1, branch0,
+    up0, down0, up1, down1, act0, slope0, act1, slope1, acc, adapted0, normed0, inv0, normed, inv, adapted1,
+    branch0,
     gb, v, grad, out0, out1, small0, small1, shifts, upd, dnd, upd0, dnd0, sems, pieces, parts,
 ):
     clips = acc.shape[0] // 256
@@ -290,38 +295,19 @@
     loads[0].wait()
 
     def begin(r):
-        rows = pl.ds(pl.multiple_of(r * 256, 256), 256)
-        adapted0[rows], normed[rows], inv[rows] = normalize(v[r], small0, r, shifts)
-
-    pl.loop(0, clips, unroll=True)(begin)
-    saves = [
-        pltpu.make_async_copy(source, target, sems.at[7 + n // 2, n % 2])
-        for n, (source, target) in enumerate(
-            ((normed, normed_hbm), (inv, inv_hbm))
-        )
-    ]
-    for copy in saves:
-        copy.start()
-    place_weights(sec, 0, *weights, up0, down0, sems.at[0], False)
-    forward_tiles(adapted0, up0, down0, small0, act0, slope0, acc)
-    for copy in saves:
-        copy.wait()
+        rows = slice(r * 256, (r + 1) * 256)
+        adapted0[rows], normed0[rows], inv0[rows] = normalize(v[r], small0, r, shifts)
 
     def between(r):
-        rows = pl.ds(pl.multiple_of(r * 256, 256), 256)
+        rows = slice(r * 256, (r + 1) * 256)
         branch = acc[rows] + small0[DOWNB : DOWNB + 1]
         branch0[rows] = branch
         result = (v[r].astype(F32) + small0[GAIN : GAIN + 1] * branch).astype(BF16)
         out0[r] = result
         adapted1[rows], normed[rows], inv[rows] = normalize(result, small1, r, shifts)
 
-    pl.loop(0, clips, unroll=True)(between)
-    place_weights(sec, 1, *weights, up1, down1, sems.at[1], False)
-    forward_tiles(adapted1, up1, down1, small1, act1, slope1, acc)
-    loads[1].wait()
-
     def top(r):
-        rows = pl.ds(pl.multiple_of(r * 256, 256), 256)
+        rows = slice(r * 256, (r + 1) * 256)
         branch = acc[rows] + small1[DOWNB : DOWNB + 1]
         gain = small1[GAIN : GAIN + 1]
         out1[r] = (out0[r].astype(F32) + gain * branch).astype(BF16)
@@ -331,7 +317,20 @@
         sums1[GAIN : GAIN + 1] += rowsum(above * branch)
         sums1[DOWNB : DOWNB + 1] += rowsum(low.astype(F32))
 
-    pl.loop(0, clips)(top)
+    begin(0)
+    place_weights(sec, 0, *weights, up0, down0, sems.at[0], False)
+    forward_tiles(
+        adapted0, up0, down0, small0, act0, slope0, acc, lambda r: begin(r) if r > 0 else None, between
+    )
+    saves = [
+        pltpu.make_async_copy(source, target, sems.at[7, n])
+        for n, (source, target) in enumerate(((normed0, normed_hbm), (inv0, inv_hbm)))
+    ]
+    for copy in saves:
+        copy.start()
+    place_weights(sec, 1, *weights, up1, down1, sems.at[1], False)
+    loads[1].wait()
+    forward_tiles(adapted1, up1, down1, small1, act1, slope1, acc, None, top)
     half_own = out_own.at[mine]
     route(sec, out0, out1, half_own, out_send, sems.at[4], True)
     for j in range(3):
@@ -380,7 +379,7 @@
     route(sec, out0, out1, half_own, out_send, sems.at[4], False)
     for n, source in enumerate((upd, dnd)):
         route_block(1, n, sec, place, source, *ends[n], parts.at[1], False)
-    for copy in tiles + [move(r) for r in range(clips)]:
+    for copy in saves + tiles + [move(r) for r in range(clips)]:
         copy.wait()
     for n, source in enumerate((upd0, dnd0)):
         route_block(0, n, sec, place, source, *ends[n], parts.at[0], False)
@@ -607,6 +606,8 @@
             pltpu.VMEM(tiled, BF16),
             pltpu.VMEM((rows, width), F32),
             pltpu.VMEM((rows, width), BF16),
+            pltpu.VMEM((rows, width), BF16),
+            pltpu.VMEM((rows, 128), F32),
             pltpu.VMEM((rows, width), BF16),
             pltpu.VMEM((rows, 128), F32),
             pltpu.VMEM((rows, width), BF16),

time: 123 us -> 124 us (level)
  no operation moved by 1% of the time
where the time goes in v2:
time: 124 us; the launch traced here: 123 us
  Pallas kernels  55.5 us (45%)
  waiting for transfers between devices  34.4 us (28%)
  starting transfers between devices  17.1 us (14%)
  other arithmetic  10.6 us (9%)
  local copies, waits for them, and re-layouts  4.22 us (3%)
    pallas_call x1, Pallas kernels, local(): pl.pallas_call(main_body, out_shape=[small_struct, small_struct, half_str...  36.2 us
    ppermute x5, waiting for transfers between devices, exchanged(): return lax.ppermute(packet, PAIR, moves)  15.6 us
    ppermute x4, waiting for transfers between devices, halved(): lax.ppermute(rows_packet, 'dp', [(i, i ^ 1 << GATHER[hop]) for i in range...  13.6 us
    pallas_call x1, Pallas kernels, local(): pl.pallas_call(last_body, grid_spec=pltpu.PrefetchScalarGridSpec(num_scal...  10 us
    ppermute x5, starting transfers between devices, exchanged(): return lax.ppermute(packet, PAIR, moves)  8.36 us
    pallas_call x9, Pallas kernels, small_call(): pl.pallas_call(body, out_shape=outs, in_specs=[SMEM] * len(scalars) + (sp...  6.9 us
    ppermute x4, starting transfers between devices, halved(): lax.ppermute(rows_packet, 'dp', [(i, i ^ 1 << GATHER[hop]) for i in range...  5.65 us
    add x4, other arithmetic, halved(): part(totals[b], first, rows) + part(latest[b], bases[b] + first, rows)  4.26 us
  transfers between devices with their start and end apart: 19, of which 9 were waited for; matrix products, arithmetic and copies ran while one was open for 11% of the time, Pallas kernels for 15%

profile of v2, /device:TPU:0, one launch (start us, length us, event | category | flops | bytes accessed | tf_op | source)
XLA Modules:
  0.0 122.8 jit_solution(6292743391719001486)
XLA Ops:
  0.6 0.6 collective-permute-start.1
  1.2 0.1 collective-permute-start.2
  1.3 2.4 %prep.1 = (f32[24,512]{1,0:T(8,128)}, f32[24,512]{1,0:T(8,128)}) custom-call(s32[1]{0:T(128)} %bitcast.sec, s32[1]{0:T(128)} %bitcast.1.place, s32[8]{0:T(128)} %speaker.1, f32[7,1,512]{2,1,0:T(1,128)} %bitcast.30, f32[1,512]{1,0:T(1,128)} %conv.1, f32[1,1536]{1,0:T(1,128)} %upb.1, f32[1,512]{1,0:T(1,128)} %downb.1, f32[1,512]{1,0:T(1,128)} %gain.1, ...), custom_call_target="tpu_custom_call" | custom-call | tf_op jit(solution)/shard_map/prep/pallas_call | solution.py:556
  3.7 0.5 collective-permute-start
  4.2 2.7 %collective-permute-done.got_small = f32[24,512]{1,0:T(8,128)} collective-permute-done((f32[24,512]{1,0:T(8,128)}, f32[24,512]{1,0:T(8,128)}, u32[]{:S(2)}, u32[]{:S(2)}) %collective-permute-start) | collective-permute-done | bytes 49184 | tf_op jit(solution)/shard_map/ppermute | solution.py:568
  6.9 36.2 %main.1 = (f32[24,512]{1,0:T(8,128)}, f32[24,512]{1,0:T(8,128)}, bf16[4,256,512]{2,1,0:T(8,128)(2,1)}, bf16[1024,512]{1,0:T(8,128)(2,1)}, f32[1024,128]{1,0:T(8,...) custom-call(s32[1]{0:T(128)} %bitcast.sec, ...), custom_call_target="tpu_custom_call" | custom-call | flops 17716740096 | bytes 25165824 | tf_op jit(solution)/shard_map/main/pallas_call | solution.py:589
  43.1 0.0 copy-start.5
  43.1 0.4 collective-permute-start.14
  43.5 0.2 collective-permute-start.11
  43.7 0.3 collective-permute-start.3
  44.0 0.2 collective-permute-start.13
  44.2 0.3 collective-permute-start.10
  44.5 1.3 %dynamic-slice_convert_fusion = f32[768,512]{1,0:T(8,128)S(1)} fusion(bf16[1536,512]{1,0:T(8,128)(2,1)} %bitcast.28, s32[]{:T(128)S(6)} %select_n.53), kind=kLoop, calls=%fused_computation.9 | loop fusion | flops 393216 | bytes 2359300 | tf_op jit(solution)/shard_map/convert_element_type | solution.py:711
  45.9 0.2 dynamic-slice_convert_fusion.1
  46.1 1.2 %fusion = bf16[768,512]{1,0:T(8,128)(2,1)} fusion(f32[768,512]{1,0:T(8,128)S(1)} %dynamic-slice_convert_fusion, bf16[8,96,512]{2,1,0:T(8,128)(2,1)S(1)} %collective-permute-done.14), kind=kLoop, calls=%fused_computation.1 | loop fusion | flops 1179648 | bytes 3145728 | tf_op jit(solution)/shard_map/convert_element_type | solution.py:718
  47.3 2.7 %collective-permute-start.15 = (bf16[768,512]{1,0:T(8,128)(2,1)}, bf16[768,512]{1,0:T(8,128)(2,1)}, u32[]{:S(2)}, u32[]{:S(2)}) collective-permute-start(bf16[768,512]{1,0:T(8,128)(2,1)} %fusion), channel_id=1, source_target_pairs={{0,1},{1,0},{2,3},{3,2},{4,5},{5,4},{6,7},{7,6},{8,9},{9,8},{10,11... | collective-permute-start | bytes 2359304 | tf_op jit(solution)/shard_map/ppermute | solution.py:701
  50.0 1.3 %fusion.1 = bf16[768,512]{1,0:T(8,128)(2,1)} fusion(f32[768,512]{1,0:T(8,128)S(1)} %dynamic-slice_convert_fusion.1, bf16[8,96,512]{2,1,0:T(8,128)(2,1)S(1)} %collective-permute-done.11), kind=kLoop, calls=%fused_computation.3 | loop fusion | flops 1179648 | bytes 3145728 | tf_op jit(solution)/shard_map/convert_element_type | solution.py:718
  51.2 10.0 %last.1 = (bf16[8,256,512]{2,1,0:T(8,128)(2,1)}, bf16[4,256,512]{2,1,0:T(8,128)(2,1)}, f32[24,512]{1,0:T(8,128)}, f32[24,512]{1,0:T(8,128)}) custom-call(s32[1]{0:T(128)} %bitcast.sec, bf16[3,1024,512]{2,1,0:T(8,128)(2,1)} %get-tuple-element.57.gpre, bf16[512,1536]{1,0:T(8,128)(2,1)} %bitcast.37, bf16[512,1536]{1,0:T(8,128)(2,1)} %collective-permute-done.1.up_got, ...), custom_call_target="tpu_custom_call" | custom-call | flops 12884901888 | bytes 12582912 | tf_op jit(solution)/shard_map/last/pallas_call | solution.py:643
  61.3 2.3 %convert_add_fusion.2 = (f32[768,512]{1,0:T(8,128)S(1)}, f32[768,512]{1,0:T(8,128)S(1)}) fusion(bf16[768,512]{1,0:T(8,128)(2,1)} %bitcast.16, bf16[1536,512]{1,0:T(8,128)(2,1)} %bitcast.29, s32[]{:T(128)S(6)} %select_n.50, bf16[768,512]{1,0:T(8,128)(2,1)} %bitcast.13, bf16[1536,512]{1,0:T(8,128)(2,1)} %bitcast.26), kind=kLoop, calls=%fused_computation.4 | loop fusion | flops 2359296 | bytes 6291460 | tf_op jit(solution)/shard_map/add | solution.py:721
  63.6 5.0 %collective-permute-done.12.refs_0_ = bf16[768,512]{1,0:T(8,128)(2,1)} collective-permute-done((bf16[768,512]{1,0:T(8,128)(2,1)}, bf16[768,512]{1,0:T(8,128)(2,1)}, u32[]{:S(2)}, u32[]{:S(2)}) %collective-permute-start.12) | collective-permute-done | bytes 786464 | tf_op jit(solution)/shard_map/ppermute | solution.py:701
  68.7 2.2 %shard_map.217 = bf16[768,512]{1,0:T(8,128)(2,1)} custom-call(s32[1]{0:T(128)} %bitcast.sec, s32[1]{0:T(128)} %bitcast.1.place, f32[768,512]{1,0:T(8,128)S(1)} %get-tuple-element.100.total0, f32[768,512]{1,0:T(8,128)S(1)} %get-tuple-element.99.total1, bf16[768,512]{1,0:T(8,128)(2,1)} %collective-permute-done.12.refs_0_, ...), custom_call_target="tpu_custom_call" | custom-call | bytes 2097152 | tf_op jit(solution)/shard_map/pallas_call | solution.py:724
  70.9 2.1 %collective-permute-start.16 = (bf16[768,512]{1,0:T(8,128)(2,1)}, bf16[768,512]{1,0:T(8,128)(2,1)}, u32[]{:S(2)}, u32[]{:S(2)}) collective-permute-start(bf16[768,512]{1,0:T(8,128)(2,1)} %shard_map.217), channel_id=1, source_target_pairs={{0,2},{1,3},{2,0},{3,1},{4,6},{5,7},{6,4},{7,5},{8,10},{9,11},{10,... | collective-permute-start | bytes 2359304 | tf_op jit(solution)/shard_map/ppermute | solution.py:701
  73.0 0.5 collective-permute-start.5
  73.5 2.6 %collective-permute-done.5.got = f32[24,512]{1,0:T(8,128)} collective-permute-done((f32[24,512]{1,0:T(8,128)S(1)}, f32[24,512]{1,0:T(8,128)}, u32[]{:S(2)}, u32[]{:S(2)}) %collective-permute-start.5) | collective-permute-done | bytes 49184 | tf_op jit(solution)/shard_map/ppermute | solution.py:680
  76.0 1.5 %shard_map.212 = (bf16[32,512]{1,0:T(8,128)(2,1)}, f32[16,512]{1,0:T(8,128)}) custom-call(s32[1]{0:T(128)} %bitcast.sec, f32[24,512]{1,0:T(8,128)} %get-tuple-element.66.own, f32[24,512]{1,0:T(8,128)} %collective-permute-done.5.got), custom_call_target="tpu_custom_call" | custom-call | bytes 2097152 | tf_op jit(solution)/shard_map/pallas_call | solution.py:724
  77.5 2.6 %collective-permute-start.6 = (bf16[32,512]{1,0:T(8,128)(2,1)}, bf16[32,512]{1,0:T(8,128)(2,1)S(1)}, u32[]{:S(2)}, u32[]{:S(2)}) collective-permute-start(bf16[32,512]{1,0:T(8,128)(2,1)} %get-tuple-element.68.before), channel_id=1, source_target_pairs={{0,8},{1,9},{2,10},{3,11},{4,12},{5,13},{6,14},{7,15},{8,0},{9,1},... | collective-permute-start | bytes 98312 | tf_op jit(solution)/shard_map/ppermute | solution.py:739
  80.1 2.8 %collective-permute-done.6.after = bf16[32,512]{1,0:T(8,128)(2,1)S(1)} collective-permute-done((bf16[32,512]{1,0:T(8,128)(2,1)}, bf16[32,512]{1,0:T(8,128)(2,1)S(1)}, u32[]{:S(2)}, u32[]{:S(2)}) %collective-permute-start.6) | collective-permute-done | bytes 32800 | tf_op jit(solution)/shard_map/ppermute | solution.py:739
  82.9 0.8 copy-done.3
  83.6 0.8 copy-done.4
  84.4 1.3 %collective-permute-start.7 = (bf16[48,512]{1,0:T(8,128)(2,1)S(1)}, bf16[48,512]{1,0:T(8,128)(2,1)S(1)}, u32[]{:S(2)}, u32[]{:S(2)}) collective-permute-start(bf16[48,512]{1,0:T(8,128)(2,1)S(1)} %get-tuple-element.70.before), channel_id=1, source_target_pairs={{0,4},{1,5},{2,6},{3,7},{4,0},{5,1},{6,2},{7,3},{8,12},{9,13},{10,... | collective-permute-start | bytes 147464 | tf_op jit(solution)/shard_map/ppermute | solution.py:739
  85.7 2.9 %collective-permute-done.7.after = bf16[48,512]{1,0:T(8,128)(2,1)S(1)} collective-permute-done((bf16[48,512]{1,0:T(8,128)(2,1)S(1)}, bf16[48,512]{1,0:T(8,128)(2,1)S(1)}, u32[]{:S(2)}, u32[]{:S(2)}) %collective-permute-start.7) | collective-permute-done | bytes 49184 | tf_op jit(solution)/shard_map/ppermute | solution.py:739
  88.6 1.6 %collective-permute-start.8 = (bf16[80,512]{1,0:T(8,128)(2,1)S(1)}, bf16[80,512]{1,0:T(8,128)(2,1)S(1)}, u32[]{:S(2)}, u32[]{:S(2)}) collective-permute-start(bf16[80,512]{1,0:T(8,128)(2,1)S(1)} %get-tuple-element.72.before), channel_id=1, source_target_pairs={{0,1},{1,0},{2,3},{3,2},{4,5},{5,4},{6,7},{7,6},{8,9},{9,8},{10,11... | collective-permute-start | bytes 245768 | tf_op jit(solution)/shard_map/ppermute | solution.py:739
  90.2 2.9 %collective-permute-done.8.after = bf16[80,512]{1,0:T(8,128)(2,1)S(1)} collective-permute-done((bf16[80,512]{1,0:T(8,128)(2,1)S(1)}, bf16[80,512]{1,0:T(8,128)(2,1)S(1)}, u32[]{:S(2)}, u32[]{:S(2)}) %collective-permute-start.8) | collective-permute-done | bytes 81952 | tf_op jit(solution)/shard_map/ppermute | solution.py:739
  93.1 0.2 collective-permute-start.9
  93.3 5.0 %collective-permute-done.9.after = bf16[144,512]{1,0:T(8,128)(2,1)S(1)} collective-permute-done((bf16[144,512]{1,0:T(8,128)(2,1)S(1)}, bf16[144,512]{1,0:T(8,128)(2,1)S(1)}, u32[]{:S(2)}, u32[]{:S(2)}) %collective-permute-start.9) | collective-permute-done | bytes 147488 | tf_op jit(solution)/shard_map/ppermute | solution.py:739
  98.3 1.1 shard_map.216
  99.4 1.3 %convert_add_fusion.4.total1 = f32[384,512]{1,0:T(8,128)S(1)} fusion(f32[768,512]{1,0:T(8,128)} %copy-done.2, s32[]{:T(128)S(6)} %select_n.52, bf16[768,512]{1,0:T(8,128)(2,1)} %collective-permute-done.15.refs_1_), kind=kLoop, calls=%fused_computation.8 | loop fusion | flops 393216 | bytes 1966084 | tf_op jit(solution)/shard_map/add | solution.py:786
  100.7 1.1 convert_add_fusion.5.total0
  101.9 1.3 %shard_map.218 = bf16[384,512]{1,0:T(8,128)(2,1)S(1)} custom-call(s32[1]{0:T(128)} %bitcast.sec, s32[1]{0:T(128)} %bitcast.1.place, f32[384,512]{1,0:T(8,128)S(1)} %convert_add_fusion.5.total0, f32[384,512]{1,0:T(8,128)S(1)} %convert_add_fusion.4.total1, bf16[768,512]{1,0:T(8,128)(2,1)} %collective-permute-done.16.refs_0_), custom_call_target="tpu_custom_call" | custom-call | bytes 2097152 | tf_op jit(solution)/shard_map/pallas_call | solution.py:724
  103.2 1.3 %collective-permute-start.17 = (bf16[384,512]{1,0:T(8,128)(2,1)S(1)}, bf16[384,512]{1,0:T(8,128)(2,1)S(1)}, u32[]{:S(2)}, u32[]{:S(2)}) collective-permute-start(bf16[384,512]{1,0:T(8,128)(2,1)S(1)} %shard_map.218), channel_id=1, source_target_pairs={{0,4},{1,5},{2,6},{3,7},{4,0},{5,1},{6,2},{7,3},{8,12},{9,13},{10,... | collective-permute-start | bytes 1179656 | tf_op jit(solution)/shard_map/ppermute | solution.py:701
  104.5 1.3 %bitcast_dynamic-update-slice_fusion.1 = bf16[1,8,256,512]{3,2,1,0:T(8,128)(2,1)S(1)} fusion(bf16[1,8,256,512]{3,2,1,0:T(8,128)(2,1)S(1)} %bitcast.31, s32[]{:T(128)S(6)} %select_n.48, bf16[4,256,512]{2,1,0:T(8,128)(2,1)} %collective-permute-done.3), kind=kLoop, calls=%fused_computation.7 | loop fusion | bytes 2097156 | tf_op jit(solution)/shard_map/dynamic_update_slice | solution.py:683
  105.9 1.7 %convert_add_fusion.6 = (f32[192,512]{1,0:T(8,128)S(1)}, f32[192,512]{1,0:T(8,128)S(1)}) fusion(f32[384,512]{1,0:T(8,128)S(1)} %convert_add_fusion.4.total1, s32[]{:T(128)S(6)} %select_n.55, bf16[768,512]{1,0:T(8,128)(2,1)} %collective-permute-done.16.refs_0_, s32[]{:T(128)S(6)} %select_n.59, s32[]{:T(128)S(6)} %select_n.56, ...), kind=kLoop, calls=%fused_computation.12 | loop fusion | flops 393216 | bytes 1966092 | tf_op jit(solution)/shard_map/add | solution.py:786
  107.6 5.5 %collective-permute-done.17.refs_0_ = bf16[384,512]{1,0:T(8,128)(2,1)S(1)} collective-permute-done((bf16[384,512]{1,0:T(8,128)(2,1)S(1)}, bf16[384,512]{1,0:T(8,128)(2,1)S(1)}, u32[]{:S(2)}, u32[]{:S(2)}) %collective-permute-start.17) | collective-permute-done | bytes 393248 | tf_op jit(solution)/shard_map/ppermute | solution.py:701
  113.2 2.3 %collective-permute-start.18 = (bf16[192,512]{1,0:T(8,128)(2,1)S(1)}, bf16[192,512]{1,0:T(8,128)(2,1)S(1)}, u32[]{:S(2)}, u32[]{:S(2)}) collective-permute-start(bf16[192,512]{1,0:T(8,128)(2,1)S(1)} %shard_map.219), channel_id=1, source_target_pairs={{0,8},{1,9},{2,10},{3,11},{4,12},{5,13},{6,14},{7,15},{8,0},{9,1},... | collective-permute-start | bytes 589832 | tf_op jit(solution)/shard_map/ppermute | solution.py:701
  115.6 1.3 %bitcast_dynamic-update-slice_fusion = bf16[1,8,256,512]{3,2,1,0:T(8,128)(2,1)S(1)} fusion(bf16[1,8,256,512]{3,2,1,0:T(8,128)(2,1)S(1)} %bitcast.32, s32[]{:T(128)S(6)} %select_n.48, bf16[4,256,512]{2,1,0:T(8,128)(2,1)} %collective-permute-done.4), kind=kLoop, calls=%fused_computation.6 | loop fusion | bytes 2097156 | tf_op jit(solution)/shard_map/dynamic_update_slice | solution.py:683
  116.9 0.1 convert_add_fusion.8
  117.0 5.0 %collective-permute-done.18.came = bf16[192,512]{1,0:T(8,128)(2,1)S(1)} collective-permute-done((bf16[192,512]{1,0:T(8,128)(2,1)S(1)}, bf16[192,512]{1,0:T(8,128)(2,1)S(1)}, u32[]{:S(2)}, u32[]{:S(2)}) %collective-permute-start.18) | collective-permute-done | bytes 196640 | tf_op jit(solution)/shard_map/ppermute | solution.py:701
  122.0 0.8 shard_map.220
  (35 shorter events, 0.1 us)
Async XLA Ops:
  0.6 6.3 %collective-permute-start.1 = (bf16[512,1536]{1,0:T(8,128)(2,1)}, bf16[512,1536]{1,0:T(8,128)(2,1)}, u32[]{:S(2)}, u32[]{:S(2)}) collective-permute-start(bf16[512,1536]{1,0:T(8,128)(2,1)} %bitcast.35), channel_id=1, source_target_pairs={{0,16},{16,0},{1,17},{17,1},{2,18},{18,2},{3,19},{19,3},{4,20},{20... | collective-permute-start | bytes 4718600 | tf_op jit(solution)/shard_map/ppermute | solution.py:570
  1.2 5.7 %collective-permute-start.2 = (bf16[1536,512]{1,0:T(8,128)(2,1)}, bf16[1536,512]{1,0:T(8,128)(2,1)}, u32[]{:S(2)}, u32[]{:S(2)}) collective-permute-start(bf16[1536,512]{1,0:T(8,128)(2,1)} %bitcast.33), channel_id=1, source_target_pairs={{0,16},{16,0},{1,17},{17,1},{2,18},{18,2},{3,19},{19,3},{4,20},{20... | collective-permute-start | bytes 4718600 | tf_op jit(solution)/shard_map/ppermute | solution.py:571
  3.7 3.2 %collective-permute-start = (f32[24,512]{1,0:T(8,128)}, f32[24,512]{1,0:T(8,128)}, u32[]{:S(2)}, u32[]{:S(2)}) collective-permute-start(f32[24,512]{1,0:T(8,128)} %get-tuple-element.54), channel_id=1, source_target_pairs={{0,16},{16,0},{1,17},{17,1},{2,18},{18,2},{3,19},{19,3},{4,20},{20... | collective-permute-start | bytes 147464 | tf_op jit(solution)/shard_map/ppermute | solution.py:568
  43.1 2.8 %copy-start.5 = (bf16[16,96,512]{2,1,0:T(8,128)(2,1)S(1)}, bf16[16,96,512]{2,1,0:T(8,128)(2,1)}, u32[]{:S(2)}) copy-start(bf16[16,96,512]{2,1,0:T(8,128)(2,1)} %get-tuple-element.80) | copy-start | bytes 4718596
  43.1 3.0 %collective-permute-start.14 = (bf16[8,96,512]{2,1,0:T(8,128)(2,1)}, bf16[8,96,512]{2,1,0:T(8,128)(2,1)S(1)}, u32[]{:S(2)}, u32[]{:S(2)}) collective-permute-start(bf16[8,96,512]{2,1,0:T(8,128)(2,1)} %get-tuple-element.89), channel_id=1, source_target_pairs={{0,16},{16,0},{1,17},{17,1},{2,18},{18,2},{3,19},{19,3},{4,20},{20... | collective-permute-start | bytes 2359304 | tf_op jit(solution)/shard_map/ppermute | solution.py:639
  43.5 6.5 %collective-permute-start.11 = (bf16[8,96,512]{2,1,0:T(8,128)(2,1)}, bf16[8,96,512]{2,1,0:T(8,128)(2,1)S(1)}, u32[]{:S(2)}, u32[]{:S(2)}) collective-permute-start(bf16[8,96,512]{2,1,0:T(8,128)(2,1)} %get-tuple-element.84), channel_id=1, source_target_pairs={{0,16},{16,0},{1,17},{17,1},{2,18},{18,2},{3,19},{19,3},{4,20},{20... | collective-permute-start | bytes 2359304 | tf_op jit(solution)/shard_map/ppermute | solution.py:639
  43.7 60.8 %collective-permute-start.3 = (bf16[4,256,512]{2,1,0:T(8,128)(2,1)}, bf16[4,256,512]{2,1,0:T(8,128)(2,1)}, u32[]{:S(2)}, u32[]{:S(2)}) collective-permute-start(bf16[4,256,512]{2,1,0:T(8,128)(2,1)} %get-tuple-element.56), channel_id=1, source_target_pairs={{0,16},{16,0},{1,17},{17,1},{2,18},{18,2},{3,19},{19,3},{4,20},{20... | collective-permute-start | bytes 3145736 | tf_op jit(solution)/shard_map/ppermute | solution.py:641
  44.0 17.3 %collective-permute-start.13 = (bf16[8,96,512]{2,1,0:T(8,128)(2,1)}, bf16[8,96,512]{2,1,0:T(8,128)(2,1)}, u32[]{:S(2)}, u32[]{:S(2)}) collective-permute-start(bf16[8,96,512]{2,1,0:T(8,128)(2,1)} %get-tuple-element.86), channel_id=1, source_target_pairs={{0,16},{16,0},{1,17},{17,1},{2,18},{18,2},{3,19},{19,3},{4,20},{20... | collective-permute-start | bytes 2359304 | tf_op jit(solution)/shard_map/ppermute | solution.py:639
  44.2 17.1 %collective-permute-start.10 = (bf16[8,96,512]{2,1,0:T(8,128)(2,1)}, bf16[8,96,512]{2,1,0:T(8,128)(2,1)}, u32[]{:S(2)}, u32[]{:S(2)}) collective-permute-start(bf16[8,96,512]{2,1,0:T(8,128)(2,1)} %get-tuple-element.81), channel_id=1, source_target_pairs={{0,16},{16,0},{1,17},{17,1},{2,18},{18,2},{3,19},{19,3},{4,20},{20... | collective-permute-start | bytes 2359304 | tf_op jit(solution)/shard_map/ppermute | solution.py:639
  47.3 16.3 %collective-permute-start.15 = (bf16[768,512]{1,0:T(8,128)(2,1)}, bf16[768,512]{1,0:T(8,128)(2,1)}, u32[]{:S(2)}, u32[]{:S(2)}) collective-permute-start(bf16[768,512]{1,0:T(8,128)(2,1)} %fusion), channel_id=1, source_target_pairs={{0,1},{1,0},{2,3},{3,2},{4,5},{5,4},{6,7},{7,6},{8,9},{9,8},{10,11... | collective-permute-start | bytes 2359304 | tf_op jit(solution)/shard_map/ppermute | solution.py:701
  51.2 17.4 %collective-permute-start.12 = (bf16[768,512]{1,0:T(8,128)(2,1)}, bf16[768,512]{1,0:T(8,128)(2,1)}, u32[]{:S(2)}, u32[]{:S(2)}) collective-permute-start(bf16[768,512]{1,0:T(8,128)(2,1)} %fusion.1), channel_id=1, source_target_pairs={{0,1},{1,0},{2,3},{3,2},{4,5},{5,4},{6,7},{7,6},{8,9},{9,8},{10,11... | collective-permute-start | bytes 2359304 | tf_op jit(solution)/shard_map/ppermute | solution.py:701
  63.6 7.3 %copy-start = (f32[768,512]{1,0:T(8,128)}, f32[768,512]{1,0:T(8,128)S(1)}, u32[]{:S(2)}) copy-start(f32[768,512]{1,0:T(8,128)S(1)} %get-tuple-element.100.total0) | copy-start | bytes 4718596
  63.6 7.3 %copy-start.2 = (f32[768,512]{1,0:T(8,128)}, f32[768,512]{1,0:T(8,128)S(1)}, u32[]{:S(2)}) copy-start(f32[768,512]{1,0:T(8,128)S(1)} %get-tuple-element.99.total1) | copy-start | bytes 4718596
  68.7 4.3 %copy-start.10 = (f32[24,512]{1,0:T(8,128)S(1)}, f32[24,512]{1,0:T(8,128)}, u32[]{:S(2)}) copy-start(f32[24,512]{1,0:T(8,128)} %get-tuple-element.67) | copy-start | bytes 147460
  70.9 31.0 %collective-permute-start.16 = (bf16[768,512]{1,0:T(8,128)(2,1)}, bf16[768,512]{1,0:T(8,128)(2,1)}, u32[]{:S(2)}, u32[]{:S(2)}) collective-permute-start(bf16[768,512]{1,0:T(8,128)(2,1)} %shard_map.217), channel_id=1, source_target_pairs={{0,2},{1,3},{2,0},{3,1},{4,6},{5,7},{6,4},{7,5},{8,10},{9,11},{10,... | collective-permute-start | bytes 2359304 | tf_op jit(solution)/shard_map/ppermute | solution.py:701
  73.0 42.6 %collective-permute-start.4 = (bf16[4,256,512]{2,1,0:T(8,128)(2,1)}, bf16[4,256,512]{2,1,0:T(8,128)(2,1)}, u32[]{:S(2)}, u32[]{:S(2)}) collective-permute-start(bf16[4,256,512]{2,1,0:T(8,128)(2,1)} %get-tuple-element.65), channel_id=1, source_target_pairs={{0,16},{16,0},{1,17},{17,1},{2,18},{18,2},{3,19},{19,3},{4,20},{20... | collective-permute-start | bytes 3145736 | tf_op jit(solution)/shard_map/ppermute | solution.py:679
  73.0 3.1 %collective-permute-start.5 = (f32[24,512]{1,0:T(8,128)S(1)}, f32[24,512]{1,0:T(8,128)}, u32[]{:S(2)}, u32[]{:S(2)}) collective-permute-start(f32[24,512]{1,0:T(8,128)S(1)} %copy-done.10), channel_id=1, source_target_pairs={{0,16},{16,0},{1,17},{17,1},{2,18},{18,2},{3,19},{19,3},{4,20},{20... | collective-permute-start | bytes 147464 | tf_op jit(solution)/shard_map/ppermute | solution.py:680
  77.5 23.2 %copy-start.1 = (f32[768,512]{1,0:T(8,128)S(1)}, f32[768,512]{1,0:T(8,128)}, u32[]{:S(2)}) copy-start(f32[768,512]{1,0:T(8,128)} %copy-done) | copy-start | bytes 4718596
  77.5 5.4 %collective-permute-start.6 = (bf16[32,512]{1,0:T(8,128)(2,1)}, bf16[32,512]{1,0:T(8,128)(2,1)S(1)}, u32[]{:S(2)}, u32[]{:S(2)}) collective-permute-start(bf16[32,512]{1,0:T(8,128)(2,1)} %get-tuple-element.68.before), channel_id=1, source_target_pairs={{0,8},{1,9},{2,10},{3,11},{4,12},{5,13},{6,14},{7,15},{8,0},{9,1},... | collective-permute-start | bytes 98312 | tf_op jit(solution)/shard_map/ppermute | solution.py:739
  82.9 0.8 copy-start.3
  83.6 0.8 copy-start.4
  84.4 4.2 %collective-permute-start.7 = (bf16[48,512]{1,0:T(8,128)(2,1)S(1)}, bf16[48,512]{1,0:T(8,128)(2,1)S(1)}, u32[]{:S(2)}, u32[]{:S(2)}) collective-permute-start(bf16[48,512]{1,0:T(8,128)(2,1)S(1)} %get-tuple-element.70.before), channel_id=1, source_target_pairs={{0,4},{1,5},{2,6},{3,7},{4,0},{5,1},{6,2},{7,3},{8,12},{9,13},{10,... | collective-permute-start | bytes 147464 | tf_op jit(solution)/shard_map/ppermute | solution.py:739
  88.6 4.5 %collective-permute-start.8 = (bf16[80,512]{1,0:T(8,128)(2,1)S(1)}, bf16[80,512]{1,0:T(8,128)(2,1)S(1)}, u32[]{:S(2)}, u32[]{:S(2)}) collective-permute-start(bf16[80,512]{1,0:T(8,128)(2,1)S(1)} %get-tuple-element.72.before), channel_id=1, source_target_pairs={{0,1},{1,0},{2,3},{3,2},{4,5},{5,4},{6,7},{7,6},{8,9},{9,8},{10,11... | collective-permute-start | bytes 245768 | tf_op jit(solution)/shard_map/ppermute | solution.py:739
  93.1 5.2 %collective-permute-start.9 = (bf16[144,512]{1,0:T(8,128)(2,1)S(1)}, bf16[144,512]{1,0:T(8,128)(2,1)S(1)}, u32[]{:S(2)}, u32[]{:S(2)}) collective-permute-start(bf16[144,512]{1,0:T(8,128)(2,1)S(1)} %get-tuple-element.74.before), channel_id=1, source_target_pairs={{0,2},{1,3},{2,0},{3,1},{4,6},{5,7},{6,4},{7,5},{8,10},{9,11},{10,... | collective-permute-start | bytes 442376 | tf_op jit(solution)/shard_map/ppermute | solution.py:739
  101.9 2.7 %copy-start.6 = (bf16[8,256,512]{2,1,0:T(8,128)(2,1)S(1)}, bf16[8,256,512]{2,1,0:T(8,128)(2,1)}, u32[]{:S(2)}) copy-start(bf16[8,256,512]{2,1,0:T(8,128)(2,1)} %get-tuple-element.55) | copy-start | bytes 6291460
  103.2 9.9 %collective-permute-start.17 = (bf16[384,512]{1,0:T(8,128)(2,1)S(1)}, bf16[384,512]{1,0:T(8,128)(2,1)S(1)}, u32[]{:S(2)}, u32[]{:S(2)}) collective-permute-start(bf16[384,512]{1,0:T(8,128)(2,1)S(1)} %shard_map.218), channel_id=1, source_target_pairs={{0,4},{1,5},{2,6},{3,7},{4,0},{5,1},{6,2},{7,3},{8,12},{9,13},{10,... | collective-permute-start | bytes 1179656 | tf_op jit(solution)/shard_map/ppermute | solution.py:701
  105.9 7.4 %copy-start.7 = (bf16[1,8,256,512]{3,2,1,0:T(8,128)(2,1)}, bf16[1,8,256,512]{3,2,1,0:T(8,128)(2,1)S(1)}, u32[]{:S(2)}) copy-start(bf16[1,8,256,512]{3,2,1,0:T(8,128)(2,1)S(1)} %bitcast_dynamic-update-slice_fusion.1) | copy-start | bytes 6291460
  105.9 9.7 %copy-start.8 = (bf16[8,256,512]{2,1,0:T(8,128)(2,1)S(1)}, bf16[8,256,512]{2,1,0:T(8,128)(2,1)}, u32[]{:S(2)}) copy-start(bf16[8,256,512]{2,1,0:T(8,128)(2,1)} %get-tuple-element.64) | copy-start | bytes 6291460
  113.2 8.7 %collective-permute-start.18 = (bf16[192,512]{1,0:T(8,128)(2,1)S(1)}, bf16[192,512]{1,0:T(8,128)(2,1)S(1)}, u32[]{:S(2)}, u32[]{:S(2)}) collective-permute-start(bf16[192,512]{1,0:T(8,128)(2,1)S(1)} %shard_map.219), channel_id=1, source_target_pairs={{0,8},{1,9},{2,10},{3,11},{4,12},{5,13},{6,14},{7,15},{8,0},{9,1},... | collective-permute-start | bytes 589832 | tf_op jit(solution)/shard_map/ppermute | solution.py:701
  116.9 5.9 %copy-start.9 = (bf16[1,8,256,512]{3,2,1,0:T(8,128)(2,1)}, bf16[1,8,256,512]{3,2,1,0:T(8,128)(2,1)S(1)}, u32[]{:S(2)}) copy-start(bf16[1,8,256,512]{3,2,1,0:T(8,128)(2,1)S(1)} %bitcast_dynamic-update-slice_fusion) | copy-start | bytes 6291460

commit v3 on v1

--- a/solution.py
+++ b/solution.py
@@ -220,14 +220,14 @@
     return 1 - ((place[0] >> ORDERS[block][0]) & 1)
 
 
-def route_block(block, layer, sec, place, sums, kept, passed, stays, sems, start):
+def route_block(block, sec, place, sums, kept, passed, stays, sems, start, rows):
     half = BLOCKS // 2
     goes = leaving(block, place)
 
     def go(*targets):
         for side, (target, first) in enumerate(zip(targets, (goes, 1 - goes))):
-            part = sums.at[pl.ds(first * half, half)]
-            copy = pltpu.make_async_copy(part, target, sems.at[layer, side])
+            part = sums.at[pl.ds(first * half, half), rows]
+            copy = pltpu.make_async_copy(part, target.at[:, rows], sems.at[side])
             copy.start() if start else copy.wait()
 
     if not start:
@@ -331,7 +331,7 @@
         sums1[GAIN : GAIN + 1] += rowsum(above * branch)
         sums1[DOWNB : DOWNB + 1] += rowsum(low.astype(F32))
 
-    pl.loop(0, clips)(top)
+    pl.loop(0, clips, unroll=True)(top)
     half_own = out_own.at[mine]
     route(sec, out0, out1, half_own, out_send, sems.at[4], True)
     for j in range(3):
@@ -343,8 +343,10 @@
         up_tile(j, ORDERS[1], adapted1, slope1[j], upd)
         down_tile(j, ORDERS[1], gb, act1[j], dnd)
     ends = ((up_keep, up_pass, up_stay), (down_keep, down_pass, down_stay))
+    share = upd.shape[1]
+    every = pl.ds(0, share)
     for n, source in enumerate((upd, dnd)):
-        route_block(1, n, sec, place, source, *ends[n], parts.at[1], True)
+        route_block(1, sec, place, source, *ends[n], parts.at[n], True, every)
 
     def move(r):
         return pltpu.make_async_copy(grad.at[r], gin1.at[r], pieces.at[r])
@@ -367,23 +369,25 @@
         sums0[DOWNB : DOWNB + 1] += rowsum(low.astype(F32))
 
     pl.loop(0, clips, unroll=True)(under)
+    for j in range(3):
+        down_tile(j, ORDERS[0], gb, act0[j], dnd0)
+    route_block(0, sec, place, dnd0, *ends[1], parts.at[2], True, every)
     tiles = []
+    thirds = [pl.ds(j * share // 3, share // 3) for j in range(3)]
     for j in range(3):
         activation_tile(j, gb, down0, slope0, sums0)
         tiles.append(pltpu.make_async_copy(slope0.at[j], gpre_hbm.at[j], sems.at[5 + j // 2 * 3, j % 2]))
         tiles[-1].start()
         up_tile(j, ORDERS[0], adapted0, slope0[j], upd0)
-    route_block(0, 0, sec, place, upd0, *ends[0], parts.at[0], True)
-    for j in range(3):
-        down_tile(j, ORDERS[0], gb, act0[j], dnd0)
-    route_block(0, 1, sec, place, dnd0, *ends[1], parts.at[0], True)
+        route_block(0, sec, place, upd0, *ends[0], parts.at[3 + j], True, thirds[j])
     route(sec, out0, out1, half_own, out_send, sems.at[4], False)
     for n, source in enumerate((upd, dnd)):
-        route_block(1, n, sec, place, source, *ends[n], parts.at[1], False)
+        route_block(1, sec, place, source, *ends[n], parts.at[n], False, every)
     for copy in tiles + [move(r) for r in range(clips)]:
         copy.wait()
-    for n, source in enumerate((upd0, dnd0)):
-        route_block(0, n, sec, place, source, *ends[n], parts.at[0], False)
+    route_block(0, sec, place, dnd0, *ends[1], parts.at[2], False, every)
+    for j in range(3):
+        route_block(0, sec, place, upd0, *ends[0], parts.at[3 + j], False, thirds[j])
 
 
 def last_body(
@@ -625,7 +629,7 @@
             pltpu.VMEM(gradient, BF16),
             pltpu.SemaphoreType.DMA((9, 2)),
             pltpu.SemaphoreType.DMA((half,)),
-            pltpu.SemaphoreType.DMA((2, 2, 2)),
+            pltpu.SemaphoreType.DMA((6, 2)),
         ],
         compiler_params=params(),
         cost_estimate=cost(11 * product, 24 << 20),

time: 123 us -> 122 us (level)
  no operation moved by 1% of the time
where the time goes in v3:
time: 122 us; the launch traced here: 121 us
  Pallas kernels  53.6 us (44%)
  waiting for transfers between devices  34.6 us (28%)
  starting transfers between devices  16.9 us (14%)
  other arithmetic  10.6 us (9%)
  local copies, waits for them, and re-layouts  4.22 us (3%)
    pallas_call x1, Pallas kernels, local(): pl.pallas_call(main_body, out_shape=[small_struct, small_struct, half_str...  34.3 us
    ppermute x5, waiting for transfers between devices, exchanged(): return lax.ppermute(packet, PAIR, moves)  15.6 us
    ppermute x4, waiting for transfers between devices, halved(): lax.ppermute(rows_packet, 'dp', [(i, i ^ 1 << GATHER[hop]) for i in range...  13.7 us
    pallas_call x1, Pallas kernels, local(): pl.pallas_call(last_body, grid_spec=pltpu.PrefetchScalarGridSpec(num_scal...  10 us
    ppermute x5, starting transfers between devices, exchanged(): return lax.ppermute(packet, PAIR, moves)  8.33 us
    pallas_call x9, Pallas kernels, small_call(): pl.pallas_call(body, out_shape=outs, in_specs=[SMEM] * len(scalars) + (sp...  6.9 us
    ppermute x4, starting transfers between devices, halved(): lax.ppermute(rows_packet, 'dp', [(i, i ^ 1 << GATHER[hop]) for i in range...  5.47 us
    add x4, other arithmetic, halved(): part(totals[b], first, rows) + part(latest[b], bases[b] + first, rows)  4.26 us
  transfers between devices with their start and end apart: 19, of which 9 were waited for; matrix products, arithmetic and copies ran while one was open for 11% of the time, Pallas kernels for 15%

profile of v3, /device:TPU:0, one launch (start us, length us, event | category | flops | bytes accessed | tf_op | source)
XLA Modules:
  0.0 121.0 jit_solution(11319809722503747742)
XLA Ops:
  0.6 0.6 collective-permute-start.1
  1.2 0.1 collective-permute-start.2
  1.3 2.4 %prep.1 = (f32[24,512]{1,0:T(8,128)}, f32[24,512]{1,0:T(8,128)}) custom-call(s32[1]{0:T(128)} %bitcast.sec, s32[1]{0:T(128)} %bitcast.1.place, s32[8]{0:T(128)} %speaker.1, f32[7,1,512]{2,1,0:T(1,128)} %bitcast.30, f32[1,512]{1,0:T(1,128)} %conv.1, f32[1,1536]{1,0:T(1,128)} %upb.1, f32[1,512]{1,0:T(1,128)} %downb.1, f32[1,512]{1,0:T(1,128)} %gain.1, ...), custom_call_target="tpu_custom_call" | custom-call | tf_op jit(solution)/shard_map/prep/pallas_call | solution.py:561
  3.7 0.5 collective-permute-start
  4.2 2.7 %collective-permute-done.got_small = f32[24,512]{1,0:T(8,128)} collective-permute-done((f32[24,512]{1,0:T(8,128)}, f32[24,512]{1,0:T(8,128)}, u32[]{:S(2)}, u32[]{:S(2)}) %collective-permute-start) | collective-permute-done | bytes 49184 | tf_op jit(solution)/shard_map/ppermute | solution.py:573
  6.9 34.3 %main.1 = (f32[24,512]{1,0:T(8,128)}, f32[24,512]{1,0:T(8,128)}, bf16[4,256,512]{2,1,0:T(8,128)(2,1)}, bf16[1024,512]{1,0:T(8,128)(2,1)}, f32[1024,128]{1,0:T(8,...) custom-call(s32[1]{0:T(128)} %bitcast.sec, ...), custom_call_target="tpu_custom_call" | custom-call | flops 17716740096 | bytes 25165824 | tf_op jit(solution)/shard_map/main/pallas_call | solution.py:594
  41.2 0.4 collective-permute-start.14
  41.7 0.1 collective-permute-start.11
  41.8 0.4 collective-permute-start.3
  42.2 0.1 collective-permute-start.13
  42.3 0.4 collective-permute-start.10
  42.7 1.3 %dynamic-slice_convert_fusion = f32[768,512]{1,0:T(8,128)S(1)} fusion(bf16[1536,512]{1,0:T(8,128)(2,1)} %bitcast.28, s32[]{:T(128)S(6)} %select_n.53), kind=kLoop, calls=%fused_computation.9 | loop fusion | flops 393216 | bytes 2359300 | tf_op jit(solution)/shard_map/convert_element_type | solution.py:714
  44.1 0.2 dynamic-slice_convert_fusion.1
  44.3 1.2 %fusion = bf16[768,512]{1,0:T(8,128)(2,1)} fusion(f32[768,512]{1,0:T(8,128)S(1)} %dynamic-slice_convert_fusion, bf16[8,96,512]{2,1,0:T(8,128)(2,1)S(1)} %collective-permute-done.14), kind=kLoop, calls=%fused_computation.1 | loop fusion | flops 1179648 | bytes 3145728 | tf_op jit(solution)/shard_map/convert_element_type | solution.py:721
  45.5 2.6 %collective-permute-start.15 = (bf16[768,512]{1,0:T(8,128)(2,1)}, bf16[768,512]{1,0:T(8,128)(2,1)}, u32[]{:S(2)}, u32[]{:S(2)}) collective-permute-start(bf16[768,512]{1,0:T(8,128)(2,1)} %fusion), channel_id=1, source_target_pairs={{0,1},{1,0},{2,3},{3,2},{4,5},{5,4},{6,7},{7,6},{8,9},{9,8},{10,11... | collective-permute-start | bytes 2359304 | tf_op jit(solution)/shard_map/ppermute | solution.py:704
  48.1 1.3 %fusion.1 = bf16[768,512]{1,0:T(8,128)(2,1)} fusion(f32[768,512]{1,0:T(8,128)S(1)} %dynamic-slice_convert_fusion.1, bf16[8,96,512]{2,1,0:T(8,128)(2,1)S(1)} %collective-permute-done.11), kind=kLoop, calls=%fused_computation.3 | loop fusion | flops 1179648 | bytes 3145728 | tf_op jit(solution)/shard_map/convert_element_type | solution.py:721
  49.4 10.0 %last.1 = (bf16[8,256,512]{2,1,0:T(8,128)(2,1)}, bf16[4,256,512]{2,1,0:T(8,128)(2,1)}, f32[24,512]{1,0:T(8,128)}, f32[24,512]{1,0:T(8,128)}) custom-call(s32[1]{0:T(128)} %bitcast.sec, bf16[3,1024,512]{2,1,0:T(8,128)(2,1)} %get-tuple-element.57.gpre, bf16[512,1536]{1,0:T(8,128)(2,1)} %bitcast.37, bf16[512,1536]{1,0:T(8,128)(2,1)} %collective-permute-done.1.up_got, ...), custom_call_target="tpu_custom_call" | custom-call | flops 12884901888 | bytes 12582912 | tf_op jit(solution)/shard_map/last/pallas_call | solution.py:646
  59.4 2.3 %convert_add_fusion.2 = (f32[768,512]{1,0:T(8,128)S(1)}, f32[768,512]{1,0:T(8,128)S(1)}) fusion(bf16[768,512]{1,0:T(8,128)(2,1)} %bitcast.16, bf16[1536,512]{1,0:T(8,128)(2,1)} %bitcast.29, s32[]{:T(128)S(6)} %select_n.50, bf16[768,512]{1,0:T(8,128)(2,1)} %bitcast.13, bf16[1536,512]{1,0:T(8,128)(2,1)} %bitcast.26), kind=kLoop, calls=%fused_computation.4 | loop fusion | flops 2359296 | bytes 6291460 | tf_op jit(solution)/shard_map/add | solution.py:724
  61.8 5.0 %collective-permute-done.12.refs_0_ = bf16[768,512]{1,0:T(8,128)(2,1)} collective-permute-done((bf16[768,512]{1,0:T(8,128)(2,1)}, bf16[768,512]{1,0:T(8,128)(2,1)}, u32[]{:S(2)}, u32[]{:S(2)}) %collective-permute-start.12) | collective-permute-done | bytes 786464 | tf_op jit(solution)/shard_map/ppermute | solution.py:704
  66.8 2.2 %shard_map.217 = bf16[768,512]{1,0:T(8,128)(2,1)} custom-call(s32[1]{0:T(128)} %bitcast.sec, s32[1]{0:T(128)} %bitcast.1.place, f32[768,512]{1,0:T(8,128)S(1)} %get-tuple-element.100.total0, f32[768,512]{1,0:T(8,128)S(1)} %get-tuple-element.99.total1, bf16[768,512]{1,0:T(8,128)(2,1)} %collective-permute-done.12.refs_0_, ...), custom_call_target="tpu_custom_call" | custom-call | bytes 2097152 | tf_op jit(solution)/shard_map/pallas_call | solution.py:727
  69.1 2.1 %collective-permute-start.16 = (bf16[768,512]{1,0:T(8,128)(2,1)}, bf16[768,512]{1,0:T(8,128)(2,1)}, u32[]{:S(2)}, u32[]{:S(2)}) collective-permute-start(bf16[768,512]{1,0:T(8,128)(2,1)} %shard_map.217), channel_id=1, source_target_pairs={{0,2},{1,3},{2,0},{3,1},{4,6},{5,7},{6,4},{7,5},{8,10},{9,11},{10,... | collective-permute-start | bytes 2359304 | tf_op jit(solution)/shard_map/ppermute | solution.py:704
  71.2 0.5 collective-permute-start.5
  71.7 2.6 %collective-permute-done.5.got = f32[24,512]{1,0:T(8,128)} collective-permute-done((f32[24,512]{1,0:T(8,128)S(1)}, f32[24,512]{1,0:T(8,128)}, u32[]{:S(2)}, u32[]{:S(2)}) %collective-permute-start.5) | collective-permute-done | bytes 49184 | tf_op jit(solution)/shard_map/ppermute | solution.py:683
  74.2 1.5 %shard_map.212 = (bf16[32,512]{1,0:T(8,128)(2,1)}, f32[16,512]{1,0:T(8,128)}) custom-call(s32[1]{0:T(128)} %bitcast.sec, f32[24,512]{1,0:T(8,128)} %get-tuple-element.66.own, f32[24,512]{1,0:T(8,128)} %collective-permute-done.5.got), custom_call_target="tpu_custom_call" | custom-call | bytes 2097152 | tf_op jit(solution)/shard_map/pallas_call | solution.py:727
  75.7 2.6 %collective-permute-start.6 = (bf16[32,512]{1,0:T(8,128)(2,1)}, bf16[32,512]{1,0:T(8,128)(2,1)S(1)}, u32[]{:S(2)}, u32[]{:S(2)}) collective-permute-start(bf16[32,512]{1,0:T(8,128)(2,1)} %get-tuple-element.68.before), channel_id=1, source_target_pairs={{0,8},{1,9},{2,10},{3,11},{4,12},{5,13},{6,14},{7,15},{8,0},{9,1},... | collective-permute-start | bytes 98312 | tf_op jit(solution)/shard_map/ppermute | solution.py:742
  78.3 2.8 %collective-permute-done.6.after = bf16[32,512]{1,0:T(8,128)(2,1)S(1)} collective-permute-done((bf16[32,512]{1,0:T(8,128)(2,1)}, bf16[32,512]{1,0:T(8,128)(2,1)S(1)}, u32[]{:S(2)}, u32[]{:S(2)}) %collective-permute-start.6) | collective-permute-done | bytes 32800 | tf_op jit(solution)/shard_map/ppermute | solution.py:742
  81.1 0.8 copy-done.3
  81.8 0.8 copy-done.4
  82.6 1.3 %collective-permute-start.7 = (bf16[48,512]{1,0:T(8,128)(2,1)S(1)}, bf16[48,512]{1,0:T(8,128)(2,1)S(1)}, u32[]{:S(2)}, u32[]{:S(2)}) collective-permute-start(bf16[48,512]{1,0:T(8,128)(2,1)S(1)} %get-tuple-element.70.before), channel_id=1, source_target_pairs={{0,4},{1,5},{2,6},{3,7},{4,0},{5,1},{6,2},{7,3},{8,12},{9,13},{10,... | collective-permute-start | bytes 147464 | tf_op jit(solution)/shard_map/ppermute | solution.py:742
  83.9 2.9 %collective-permute-done.7.after = bf16[48,512]{1,0:T(8,128)(2,1)S(1)} collective-permute-done((bf16[48,512]{1,0:T(8,128)(2,1)S(1)}, bf16[48,512]{1,0:T(8,128)(2,1)S(1)}, u32[]{:S(2)}, u32[]{:S(2)}) %collective-permute-start.7) | collective-permute-done | bytes 49184 | tf_op jit(solution)/shard_map/ppermute | solution.py:742
  86.8 1.5 %collective-permute-start.8 = (bf16[80,512]{1,0:T(8,128)(2,1)S(1)}, bf16[80,512]{1,0:T(8,128)(2,1)S(1)}, u32[]{:S(2)}, u32[]{:S(2)}) collective-permute-start(bf16[80,512]{1,0:T(8,128)(2,1)S(1)} %get-tuple-element.72.before), channel_id=1, source_target_pairs={{0,1},{1,0},{2,3},{3,2},{4,5},{5,4},{6,7},{7,6},{8,9},{9,8},{10,11... | collective-permute-start | bytes 245768 | tf_op jit(solution)/shard_map/ppermute | solution.py:742
  88.3 3.0 %collective-permute-done.8.after = bf16[80,512]{1,0:T(8,128)(2,1)S(1)} collective-permute-done((bf16[80,512]{1,0:T(8,128)(2,1)S(1)}, bf16[80,512]{1,0:T(8,128)(2,1)S(1)}, u32[]{:S(2)}, u32[]{:S(2)}) %collective-permute-start.8) | collective-permute-done | bytes 81952 | tf_op jit(solution)/shard_map/ppermute | solution.py:742
  91.3 0.1 collective-permute-start.9
  91.4 5.1 %collective-permute-done.9.after = bf16[144,512]{1,0:T(8,128)(2,1)S(1)} collective-permute-done((bf16[144,512]{1,0:T(8,128)(2,1)S(1)}, bf16[144,512]{1,0:T(8,128)(2,1)S(1)}, u32[]{:S(2)}, u32[]{:S(2)}) %collective-permute-start.9) | collective-permute-done | bytes 147488 | tf_op jit(solution)/shard_map/ppermute | solution.py:742
  96.5 1.1 shard_map.216
  97.6 1.3 %convert_add_fusion.4.total1 = f32[384,512]{1,0:T(8,128)S(1)} fusion(f32[768,512]{1,0:T(8,128)} %copy-done.2, s32[]{:T(128)S(6)} %select_n.52, bf16[768,512]{1,0:T(8,128)(2,1)} %collective-permute-done.15.refs_1_), kind=kLoop, calls=%fused_computation.8 | loop fusion | flops 393216 | bytes 1966084 | tf_op jit(solution)/shard_map/add | solution.py:789
  98.9 1.1 convert_add_fusion.5.total0
  100.1 0.0 copy-start.6
  100.1 1.3 %shard_map.218 = bf16[384,512]{1,0:T(8,128)(2,1)S(1)} custom-call(s32[1]{0:T(128)} %bitcast.sec, s32[1]{0:T(128)} %bitcast.1.place, f32[384,512]{1,0:T(8,128)S(1)} %convert_add_fusion.5.total0, f32[384,512]{1,0:T(8,128)S(1)} %convert_add_fusion.4.total1, bf16[768,512]{1,0:T(8,128)(2,1)} %collective-permute-done.16.refs_0_), custom_call_target="tpu_custom_call" | custom-call | bytes 2097152 | tf_op jit(solution)/shard_map/pallas_call | solution.py:727
  101.4 1.3 %collective-permute-start.17 = (bf16[384,512]{1,0:T(8,128)(2,1)S(1)}, bf16[384,512]{1,0:T(8,128)(2,1)S(1)}, u32[]{:S(2)}, u32[]{:S(2)}) collective-permute-start(bf16[384,512]{1,0:T(8,128)(2,1)S(1)} %shard_map.218), channel_id=1, source_target_pairs={{0,4},{1,5},{2,6},{3,7},{4,0},{5,1},{6,2},{7,3},{8,12},{9,13},{10,... | collective-permute-start | bytes 1179656 | tf_op jit(solution)/shard_map/ppermute | solution.py:704
  102.7 1.3 %bitcast_dynamic-update-slice_fusion.1 = bf16[1,8,256,512]{3,2,1,0:T(8,128)(2,1)S(1)} fusion(bf16[1,8,256,512]{3,2,1,0:T(8,128)(2,1)S(1)} %bitcast.31, s32[]{:T(128)S(6)} %select_n.48, bf16[4,256,512]{2,1,0:T(8,128)(2,1)} %collective-permute-done.3), kind=kLoop, calls=%fused_computation.7 | loop fusion | bytes 2097156 | tf_op jit(solution)/shard_map/dynamic_update_slice | solution.py:686
  104.1 1.7 %convert_add_fusion.6 = (f32[192,512]{1,0:T(8,128)S(1)}, f32[192,512]{1,0:T(8,128)S(1)}) fusion(f32[384,512]{1,0:T(8,128)S(1)} %convert_add_fusion.4.total1, s32[]{:T(128)S(6)} %select_n.55, bf16[768,512]{1,0:T(8,128)(2,1)} %collective-permute-done.16.refs_0_, s32[]{:T(128)S(6)} %select_n.59, s32[]{:T(128)S(6)} %select_n.56, ...), kind=kLoop, calls=%fused_computation.12 | loop fusion | flops 393216 | bytes 1966092 | tf_op jit(solution)/shard_map/add | solution.py:789
  105.8 5.5 %collective-permute-done.17.refs_0_ = bf16[384,512]{1,0:T(8,128)(2,1)S(1)} collective-permute-done((bf16[384,512]{1,0:T(8,128)(2,1)S(1)}, bf16[384,512]{1,0:T(8,128)(2,1)S(1)}, u32[]{:S(2)}, u32[]{:S(2)}) %collective-permute-start.17) | collective-permute-done | bytes 393248 | tf_op jit(solution)/shard_map/ppermute | solution.py:704
  111.4 2.3 %collective-permute-start.18 = (bf16[192,512]{1,0:T(8,128)(2,1)S(1)}, bf16[192,512]{1,0:T(8,128)(2,1)S(1)}, u32[]{:S(2)}, u32[]{:S(2)}) collective-permute-start(bf16[192,512]{1,0:T(8,128)(2,1)S(1)} %shard_map.219), channel_id=1, source_target_pairs={{0,8},{1,9},{2,10},{3,11},{4,12},{5,13},{6,14},{7,15},{8,0},{9,1},... | collective-permute-start | bytes 589832 | tf_op jit(solution)/shard_map/ppermute | solution.py:704
  113.7 1.3 %bitcast_dynamic-update-slice_fusion = bf16[1,8,256,512]{3,2,1,0:T(8,128)(2,1)S(1)} fusion(bf16[1,8,256,512]{3,2,1,0:T(8,128)(2,1)S(1)} %bitcast.32, s32[]{:T(128)S(6)} %select_n.48, bf16[4,256,512]{2,1,0:T(8,128)(2,1)} %collective-permute-done.4), kind=kLoop, calls=%fused_computation.6 | loop fusion | bytes 2097156 | tf_op jit(solution)/shard_map/dynamic_update_slice | solution.py:686
  115.1 0.1 convert_add_fusion.8
  115.2 5.0 %collective-permute-done.18.came = bf16[192,512]{1,0:T(8,128)(2,1)S(1)} collective-permute-done((bf16[192,512]{1,0:T(8,128)(2,1)S(1)}, bf16[192,512]{1,0:T(8,128)(2,1)S(1)}, u32[]{:S(2)}, u32[]{:S(2)}) %collective-permute-start.18) | collective-permute-done | bytes 196640 | tf_op jit(solution)/shard_map/ppermute | solution.py:704
  120.2 0.8 shard_map.220
  (35 shorter events, 0.1 us)
Async XLA Ops:
  0.6 6.3 %collective-permute-start.1 = (bf16[512,1536]{1,0:T(8,128)(2,1)}, bf16[512,1536]{1,0:T(8,128)(2,1)}, u32[]{:S(2)}, u32[]{:S(2)}) collective-permute-start(bf16[512,1536]{1,0:T(8,128)(2,1)} %bitcast.35), channel_id=1, source_target_pairs={{0,16},{16,0},{1,17},{17,1},{2,18},{18,2},{3,19},{19,3},{4,20},{20... | collective-permute-start | bytes 4718600 | tf_op jit(solution)/shard_map/ppermute | solution.py:575
  1.2 5.7 %collective-permute-start.2 = (bf16[1536,512]{1,0:T(8,128)(2,1)}, bf16[1536,512]{1,0:T(8,128)(2,1)}, u32[]{:S(2)}, u32[]{:S(2)}) collective-permute-start(bf16[1536,512]{1,0:T(8,128)(2,1)} %bitcast.33), channel_id=1, source_target_pairs={{0,16},{16,0},{1,17},{17,1},{2,18},{18,2},{3,19},{19,3},{4,20},{20... | collective-permute-start | bytes 4718600 | tf_op jit(solution)/shard_map/ppermute | solution.py:576
  3.7 3.2 %collective-permute-start = (f32[24,512]{1,0:T(8,128)}, f32[24,512]{1,0:T(8,128)}, u32[]{:S(2)}, u32[]{:S(2)}) collective-permute-start(f32[24,512]{1,0:T(8,128)} %get-tuple-element.54), channel_id=1, source_target_pairs={{0,16},{16,0},{1,17},{17,1},{2,18},{18,2},{3,19},{19,3},{4,20},{20... | collective-permute-start | bytes 147464 | tf_op jit(solution)/shard_map/ppermute | solution.py:573
  41.2 2.8 %copy-start.5 = (bf16[16,96,512]{2,1,0:T(8,128)(2,1)S(1)}, bf16[16,96,512]{2,1,0:T(8,128)(2,1)}, u32[]{:S(2)}) copy-start(bf16[16,96,512]{2,1,0:T(8,128)(2,1)} %get-tuple-element.80) | copy-start | bytes 4718596
  41.2 3.0 %collective-permute-start.14 = (bf16[8,96,512]{2,1,0:T(8,128)(2,1)}, bf16[8,96,512]{2,1,0:T(8,128)(2,1)S(1)}, u32[]{:S(2)}, u32[]{:S(2)}) collective-permute-start(bf16[8,96,512]{2,1,0:T(8,128)(2,1)} %get-tuple-element.89), channel_id=1, source_target_pairs={{0,16},{16,0},{1,17},{17,1},{2,18},{18,2},{3,19},{19,3},{4,20},{20... | collective-permute-start | bytes 2359304 | tf_op jit(solution)/shard_map/ppermute | solution.py:642
  41.7 6.5 %collective-permute-start.11 = (bf16[8,96,512]{2,1,0:T(8,128)(2,1)}, bf16[8,96,512]{2,1,0:T(8,128)(2,1)S(1)}, u32[]{:S(2)}, u32[]{:S(2)}) collective-permute-start(bf16[8,96,512]{2,1,0:T(8,128)(2,1)} %get-tuple-element.84), channel_id=1, source_target_pairs={{0,16},{16,0},{1,17},{17,1},{2,18},{18,2},{3,19},{19,3},{4,20},{20... | collective-permute-start | bytes 2359304 | tf_op jit(solution)/shard_map/ppermute | solution.py:642
  41.8 60.9 %collective-permute-start.3 = (bf16[4,256,512]{2,1,0:T(8,128)(2,1)}, bf16[4,256,512]{2,1,0:T(8,128)(2,1)}, u32[]{:S(2)}, u32[]{:S(2)}) collective-permute-start(bf16[4,256,512]{2,1,0:T(8,128)(2,1)} %get-tuple-element.56), channel_id=1, source_target_pairs={{0,16},{16,0},{1,17},{17,1},{2,18},{18,2},{3,19},{19,3},{4,20},{20... | collective-permute-start | bytes 3145736 | tf_op jit(solution)/shard_map/ppermute | solution.py:644
  42.2 17.2 %collective-permute-start.13 = (bf16[8,96,512]{2,1,0:T(8,128)(2,1)}, bf16[8,96,512]{2,1,0:T(8,128)(2,1)}, u32[]{:S(2)}, u32[]{:S(2)}) collective-permute-start(bf16[8,96,512]{2,1,0:T(8,128)(2,1)} %get-tuple-element.86), channel_id=1, source_target_pairs={{0,16},{16,0},{1,17},{17,1},{2,18},{18,2},{3,19},{19,3},{4,20},{20... | collective-permute-start | bytes 2359304 | tf_op jit(solution)/shard_map/ppermute | solution.py:642
  42.3 17.1 %collective-permute-start.10 = (bf16[8,96,512]{2,1,0:T(8,128)(2,1)}, bf16[8,96,512]{2,1,0:T(8,128)(2,1)}, u32[]{:S(2)}, u32[]{:S(2)}) collective-permute-start(bf16[8,96,512]{2,1,0:T(8,128)(2,1)} %get-tuple-element.81), channel_id=1, source_target_pairs={{0,16},{16,0},{1,17},{17,1},{2,18},{18,2},{3,19},{19,3},{4,20},{20... | collective-permute-start | bytes 2359304 | tf_op jit(solution)/shard_map/ppermute | solution.py:642
  45.5 16.3 %collective-permute-start.15 = (bf16[768,512]{1,0:T(8,128)(2,1)}, bf16[768,512]{1,0:T(8,128)(2,1)}, u32[]{:S(2)}, u32[]{:S(2)}) collective-permute-start(bf16[768,512]{1,0:T(8,128)(2,1)} %fusion), channel_id=1, source_target_pairs={{0,1},{1,0},{2,3},{3,2},{4,5},{5,4},{6,7},{7,6},{8,9},{9,8},{10,11... | collective-permute-start | bytes 2359304 | tf_op jit(solution)/shard_map/ppermute | solution.py:704
  49.4 17.4 %collective-permute-start.12 = (bf16[768,512]{1,0:T(8,128)(2,1)}, bf16[768,512]{1,0:T(8,128)(2,1)}, u32[]{:S(2)}, u32[]{:S(2)}) collective-permute-start(bf16[768,512]{1,0:T(8,128)(2,1)} %fusion.1), channel_id=1, source_target_pairs={{0,1},{1,0},{2,3},{3,2},{4,5},{5,4},{6,7},{7,6},{8,9},{9,8},{10,11... | collective-permute-start | bytes 2359304 | tf_op jit(solution)/shard_map/ppermute | solution.py:704
  61.8 7.3 %copy-start = (f32[768,512]{1,0:T(8,128)}, f32[768,512]{1,0:T(8,128)S(1)}, u32[]{:S(2)}) copy-start(f32[768,512]{1,0:T(8,128)S(1)} %get-tuple-element.100.total0) | copy-start | bytes 4718596
  61.8 7.3 %copy-start.2 = (f32[768,512]{1,0:T(8,128)}, f32[768,512]{1,0:T(8,128)S(1)}, u32[]{:S(2)}) copy-start(f32[768,512]{1,0:T(8,128)S(1)} %get-tuple-element.99.total1) | copy-start | bytes 4718596
  66.8 4.3 %copy-start.10 = (f32[24,512]{1,0:T(8,128)S(1)}, f32[24,512]{1,0:T(8,128)}, u32[]{:S(2)}) copy-start(f32[24,512]{1,0:T(8,128)} %get-tuple-element.67) | copy-start | bytes 147460
  69.1 31.0 %collective-permute-start.16 = (bf16[768,512]{1,0:T(8,128)(2,1)}, bf16[768,512]{1,0:T(8,128)(2,1)}, u32[]{:S(2)}, u32[]{:S(2)}) collective-permute-start(bf16[768,512]{1,0:T(8,128)(2,1)} %shard_map.217), channel_id=1, source_target_pairs={{0,2},{1,3},{2,0},{3,1},{4,6},{5,7},{6,4},{7,5},{8,10},{9,11},{10,... | collective-permute-start | bytes 2359304 | tf_op jit(solution)/shard_map/ppermute | solution.py:704
  71.2 42.6 %collective-permute-start.4 = (bf16[4,256,512]{2,1,0:T(8,128)(2,1)}, bf16[4,256,512]{2,1,0:T(8,128)(2,1)}, u32[]{:S(2)}, u32[]{:S(2)}) collective-permute-start(bf16[4,256,512]{2,1,0:T(8,128)(2,1)} %get-tuple-element.65), channel_id=1, source_target_pairs={{0,16},{16,0},{1,17},{17,1},{2,18},{18,2},{3,19},{19,3},{4,20},{20... | collective-permute-start | bytes 3145736 | tf_op jit(solution)/shard_map/ppermute | solution.py:682
  71.2 3.1 %collective-permute-start.5 = (f32[24,512]{1,0:T(8,128)S(1)}, f32[24,512]{1,0:T(8,128)}, u32[]{:S(2)}, u32[]{:S(2)}) collective-permute-start(f32[24,512]{1,0:T(8,128)S(1)} %copy-done.10), channel_id=1, source_target_pairs={{0,16},{16,0},{1,17},{17,1},{2,18},{18,2},{3,19},{19,3},{4,20},{20... | collective-permute-start | bytes 147464 | tf_op jit(solution)/shard_map/ppermute | solution.py:683
  75.7 23.2 %copy-start.1 = (f32[768,512]{1,0:T(8,128)S(1)}, f32[768,512]{1,0:T(8,128)}, u32[]{:S(2)}) copy-start(f32[768,512]{1,0:T(8,128)} %copy-done) | copy-start | bytes 4718596
  75.7 5.4 %collective-permute-start.6 = (bf16[32,512]{1,0:T(8,128)(2,1)}, bf16[32,512]{1,0:T(8,128)(2,1)S(1)}, u32[]{:S(2)}, u32[]{:S(2)}) collective-permute-start(bf16[32,512]{1,0:T(8,128)(2,1)} %get-tuple-element.68.before), channel_id=1, source_target_pairs={{0,8},{1,9},{2,10},{3,11},{4,12},{5,13},{6,14},{7,15},{8,0},{9,1},... | collective-permute-start | bytes 98312 | tf_op jit(solution)/shard_map/ppermute | solution.py:742
  81.1 0.8 copy-start.3
  81.8 0.8 copy-start.4
  82.6 4.2 %collective-permute-start.7 = (bf16[48,512]{1,0:T(8,128)(2,1)S(1)}, bf16[48,512]{1,0:T(8,128)(2,1)S(1)}, u32[]{:S(2)}, u32[]{:S(2)}) collective-permute-start(bf16[48,512]{1,0:T(8,128)(2,1)S(1)} %get-tuple-element.70.before), channel_id=1, source_target_pairs={{0,4},{1,5},{2,6},{3,7},{4,0},{5,1},{6,2},{7,3},{8,12},{9,13},{10,... | collective-permute-start | bytes 147464 | tf_op jit(solution)/shard_map/ppermute | solution.py:742
  86.8 4.5 %collective-permute-start.8 = (bf16[80,512]{1,0:T(8,128)(2,1)S(1)}, bf16[80,512]{1,0:T(8,128)(2,1)S(1)}, u32[]{:S(2)}, u32[]{:S(2)}) collective-permute-start(bf16[80,512]{1,0:T(8,128)(2,1)S(1)} %get-tuple-element.72.before), channel_id=1, source_target_pairs={{0,1},{1,0},{2,3},{3,2},{4,5},{5,4},{6,7},{7,6},{8,9},{9,8},{10,11... | collective-permute-start | bytes 245768 | tf_op jit(solution)/shard_map/ppermute | solution.py:742
  91.3 5.2 %collective-permute-start.9 = (bf16[144,512]{1,0:T(8,128)(2,1)S(1)}, bf16[144,512]{1,0:T(8,128)(2,1)S(1)}, u32[]{:S(2)}, u32[]{:S(2)}) collective-permute-start(bf16[144,512]{1,0:T(8,128)(2,1)S(1)} %get-tuple-element.74.before), channel_id=1, source_target_pairs={{0,2},{1,3},{2,0},{3,1},{4,6},{5,7},{6,4},{7,5},{8,10},{9,11},{10,... | collective-permute-start | bytes 442376 | tf_op jit(solution)/shard_map/ppermute | solution.py:742
  100.1 2.7 %copy-start.6 = (bf16[8,256,512]{2,1,0:T(8,128)(2,1)S(1)}, bf16[8,256,512]{2,1,0:T(8,128)(2,1)}, u32[]{:S(2)}) copy-start(bf16[8,256,512]{2,1,0:T(8,128)(2,1)} %get-tuple-element.55) | copy-start | bytes 6291460
  101.4 9.9 %collective-permute-start.17 = (bf16[384,512]{1,0:T(8,128)(2,1)S(1)}, bf16[384,512]{1,0:T(8,128)(2,1)S(1)}, u32[]{:S(2)}, u32[]{:S(2)}) collective-permute-start(bf16[384,512]{1,0:T(8,128)(2,1)S(1)} %shard_map.218), channel_id=1, source_target_pairs={{0,4},{1,5},{2,6},{3,7},{4,0},{5,1},{6,2},{7,3},{8,12},{9,13},{10,... | collective-permute-start | bytes 1179656 | tf_op jit(solution)/shard_map/ppermute | solution.py:704
  104.1 7.4 %copy-start.7 = (bf16[1,8,256,512]{3,2,1,0:T(8,128)(2,1)}, bf16[1,8,256,512]{3,2,1,0:T(8,128)(2,1)S(1)}, u32[]{:S(2)}) copy-start(bf16[1,8,256,512]{3,2,1,0:T(8,128)(2,1)S(1)} %bitcast_dynamic-update-slice_fusion.1) | copy-start | bytes 6291460
  104.1 9.7 %copy-start.8 = (bf16[8,256,512]{2,1,0:T(8,128)(2,1)S(1)}, bf16[8,256,512]{2,1,0:T(8,128)(2,1)}, u32[]{:S(2)}) copy-start(bf16[8,256,512]{2,1,0:T(8,128)(2,1)} %get-tuple-element.64) | copy-start | bytes 6291460
  111.4 8.7 %collective-permute-start.18 = (bf16[192,512]{1,0:T(8,128)(2,1)S(1)}, bf16[192,512]{1,0:T(8,128)(2,1)S(1)}, u32[]{:S(2)}, u32[]{:S(2)}) collective-permute-start(bf16[192,512]{1,0:T(8,128)(2,1)S(1)} %shard_map.219), channel_id=1, source_target_pairs={{0,8},{1,9},{2,10},{3,11},{4,12},{5,13},{6,14},{7,15},{8,0},{9,1},... | collective-permute-start | bytes 589832 | tf_op jit(solution)/shard_map/ppermute | solution.py:704
  115.1 5.9 %copy-start.9 = (bf16[1,8,256,512]{3,2,1,0:T(8,128)(2,1)}, bf16[1,8,256,512]{3,2,1,0:T(8,128)(2,1)S(1)}, u32[]{:S(2)}) copy-start(bf16[1,8,256,512]{3,2,1,0:T(8,128)(2,1)S(1)} %bitcast_dynamic-update-slice_fusion) | copy-start | bytes 6291460
